TPU v7x, 32 devices: a whole 2x2x4 slice. The times are simulated.
32 devices in a mesh: frames: 16 (over z, y, core), text: 2 (over x).
Axes of the slice: x: 2, y: 2, z: 4, core: 2. Of those that a mesh axis runs over, the one named last changes fastest.
Arguments:
- frames_in: bfloat16 [32768, 768], P(('frames', 'text')), may hold values from -6 to 6
- frame_item: int32 [32, 1024], P('frames'), may hold values from 0 to 3, never falling along the last dimension, each value on 1 to 512 neighbouring positions
- text_in: bfloat16 [128, 256, 768], P('frames', 'text'), may hold values from -6 to 6
- text_len: int32 [128], P('frames'), may hold values from 77 to 256
- time_embed: bfloat16 [128, 768], P(('frames', 'text')), may hold values from -6 to 6
- cotangent: bfloat16 [32768, 768], P(('frames', 'text')), may hold values from -6 to 6
- w_mod: bfloat16 [768, 6144], replicated, may hold values from -0.21875 to 0.21875
- b_mod: bfloat16 [6144], replicated, may hold values from -1.75 to 1.75
- w_qkv: bfloat16 [768, 2304], replicated, may hold values from -0.21875 to 0.21875
- w_out: bfloat16 [768, 768], replicated, may hold values from -0.625 to 0.625
- b_out: bfloat16 [768], replicated, may hold values from -1.75 to 1.75
- w_q_cross: bfloat16 [768, 768], replicated, may hold values from -0.21875 to 0.21875
- w_kv_cross: bfloat16 [768, 1536], replicated, may hold values from -0.21875 to 0.21875
- w_out_cross: bfloat16 [768, 768], replicated, may hold values from -0.625 to 0.625
- b_out_cross: bfloat16 [768], replicated, may hold values from -1.75 to 1.75
- w_up: bfloat16 [768, 3072], replicated, may hold values from -0.21875 to 0.21875
- b_up: bfloat16 [3072], replicated, may hold values from -1.75 to 1.75
- w_down: bfloat16 [3072, 768], replicated, may hold values from -0.109375 to 0.109375
- b_down: bfloat16 [768], replicated, may hold values from -1.75 to 1.75
Outputs:
- frames_out: float32 [32768, 768], P(('frames', 'text'))
- frames_grad: float32 [32768, 768], P(('frames', 'text'))
- text_grad: float32 [128, 256, 768], P('frames', 'text')
- time_grad: float32 [128, 768], P(('frames', 'text'))
- grad_w_mod: float32 [768, 6144], P('frames')
- grad_b_mod: float32 [6144], P('frames')
- grad_w_qkv: float32 [768, 2304], P('frames')
- grad_w_out: float32 [768, 768], P('frames')
- grad_b_out: float32 [768], P('frames')
- grad_w_q_cross: float32 [768, 768], P('frames')
- grad_w_kv_cross: float32 [768, 1536], P('frames')
- grad_w_out_cross: float32 [768, 768], P('frames')
- grad_b_out_cross: float32 [768], P('frames')
- grad_w_up: float32 [768, 3072], P('frames')
- grad_b_up: float32 [3072], P('frames')
- grad_w_down: float32 [3072, 768], P('frames')
- grad_b_down: float32 [768], P('frames')
Inputs may be any that keep to these rules, and one draw needn't show every extreme that they name: `frame_item`: in each row of 1024 frames the item numbers never fall; each of the 4 items holds 1 to 512 frames, one exactly 512.
All inputs are finite; a program needn't handle non-finite values.
Results may differ from a plain program's by a relative error of at most 0.03.
Values may be sent and summed in bfloat16 or wider, within the bound.
A program may use at most 384 MiB of HBM per device.

v0:
```python
import jax
import jax.numpy as jnp
from jax import lax
from jax.sharding import PartitionSpec as P

HEAD_DIM = 64


epsilon = 1e-06
masked_add = -1000000000.0
highest = lax.Precision.HIGHEST


def swapped(value, axis, stride):
    mask = 2**stride
    pairs = [(source, source ^ mask) for source in range(lax.axis_size(axis))]
    return lax.ppermute(value, axis, pairs)


def rows_dot(left_side, right_side):
    return jnp.dot(left_side, right_side, preferred_element_type=jnp.float32)


def left_dot(left_side, right_side):
    return lax.dot_general(
        left_side, right_side, (((0,), (0,)), ((), ())), preferred_element_type=jnp.float32
    )


def right_dot(left_side, right_side):
    return lax.dot_general(
        left_side, right_side, (((1,), (1,)), ((), ())), preferred_element_type=jnp.float32
    )


def layer_norm(values):
    center = values - jnp.mean(values, axis=-1, keepdims=True)
    spread = jnp.mean(center * center, axis=-1, keepdims=True)
    return center * lax.rsqrt(spread + epsilon)


def modulate(values, shift_by, scale_by):
    return layer_norm(values) * (1.0 + scale_by) + shift_by


def gelu_tanh(inputs):
    return (
        0.5
        * inputs
        * (1.0 + jnp.tanh(0.7978845608028654 * (inputs + 0.044715 * inputs * inputs * inputs)))
    )


def self_scores(query_rows, segment_rows, key_rows, segment, score_scale):
    scores = (
        jnp.einsum("qhd,khd->hqk", query_rows, key_rows, preferred_element_type=jnp.float32)
        * score_scale
    )
    return scores + jnp.where(segment_rows[:, None] == segment[None, :], 0.0, masked_add)[None]


def self_forward(queries, key_rows, value_rows, segment, score_scale):
    row_count, head_count, head_size = queries.shape
    block_rows = min(512, row_count)
    block_count = row_count // block_rows

    def one_block(inputs):
        query_rows, segment_rows = inputs
        scores = self_scores(query_rows, segment_rows, key_rows, segment, score_scale)
        maximum = jnp.max(scores, axis=-1, keepdims=True)
        exponent = jnp.exp(scores - maximum)
        totals = jnp.sum(exponent, axis=-1, keepdims=True)
        prob_low = (exponent / totals).astype(jnp.bfloat16)
        attended = jnp.einsum(
            "hqk,khd->qhd", prob_low, value_rows, preferred_element_type=jnp.float32
        )
        return (attended, (maximum + jnp.log(totals))[..., 0])

    attended, log_total = lax.map(
        one_block,
        (
            queries.reshape(block_count, block_rows, head_count, head_size),
            segment.reshape(block_count, block_rows),
        ),
    )
    return (attended.reshape(row_count, head_count * head_size), log_total)


def self_backward(queries, key_rows, value_rows, segment, grad_attended, log_total, score_scale):
    row_count, head_count, head_size = queries.shape
    block_rows = min(512, row_count)
    block_count = row_count // block_rows

    def one_block(running, inputs):
        grad_keys, grad_values = running
        query_rows, segment_rows, grad_rows, log_rows = inputs
        scores = self_scores(query_rows, segment_rows, key_rows, segment, score_scale)
        prob_full = jnp.exp(scores - log_rows[..., None])
        prob_low = prob_full.astype(jnp.bfloat16)
        grad_prob = jnp.einsum(
            "qhd,khd->hqk", grad_rows, value_rows, preferred_element_type=jnp.float32
        )
        row_delta = jnp.sum(prob_full * grad_prob, axis=-1, keepdims=True)
        grad_scores = (prob_full * (grad_prob - row_delta)).astype(jnp.bfloat16)
        grad_query = (
            jnp.einsum("hqk,khd->qhd", grad_scores, key_rows, preferred_element_type=jnp.float32)
            * score_scale
        )
        grad_keys = (
            grad_keys
            + jnp.einsum(
                "hqk,qhd->khd", grad_scores, query_rows, preferred_element_type=jnp.float32
            )
            * score_scale
        )
        grad_values = grad_values + jnp.einsum(
            "hqk,qhd->khd", prob_low, grad_rows, preferred_element_type=jnp.float32
        )
        return ((grad_keys, grad_values), grad_query)

    zeros_start = jnp.zeros((row_count, head_count, head_size), jnp.float32)
    inputs = (
        queries.reshape(block_count, block_rows, head_count, head_size),
        segment.reshape(block_count, block_rows),
        grad_attended.reshape(block_count, block_rows, head_count, head_size),
        log_total,
    )
    (grad_keys, grad_values), grad_query = lax.scan(one_block, (zeros_start, zeros_start), inputs)
    return (grad_query.reshape(row_count, head_count, head_size), grad_keys, grad_values)


def cross_split(text_kv, head_count, head_size):
    item_count, token_span, doubled = text_kv.shape
    key_rows = text_kv[:, :, : doubled // 2].reshape(item_count, token_span, head_count, head_size)
    value_rows = text_kv[:, :, doubled // 2 :].reshape(
        item_count, token_span, head_count, head_size
    )
    return (key_rows, value_rows)


def cross_scores(queries, segment, key_rows, lengths, half_index, score_scale):
    item_count, token_span = (key_rows.shape[0], key_rows.shape[1])
    scores = (
        jnp.einsum("qhd,ijhd->hqij", queries, key_rows, preferred_element_type=jnp.float32)
        * score_scale
    )
    position = half_index * token_span + jnp.arange(token_span, dtype=jnp.int32)
    item_ids = jnp.arange(item_count, dtype=jnp.int32)
    valid_key = (segment[:, None, None] == item_ids[None, :, None]) & (
        position[None, None, :] < lengths[None, :, None]
    )
    return scores + jnp.where(valid_key, 0.0, masked_add)[None]


def cross_forward(queries, segment, text_kv, lengths, half_index, score_scale):
    key_rows, value_rows = cross_split(text_kv, queries.shape[1], queries.shape[2])
    scores = cross_scores(queries, segment, key_rows, lengths, half_index, score_scale)
    maximum = jnp.max(scores, axis=(2, 3))
    exponent = jnp.exp(scores - maximum[:, :, None, None])
    totals = jnp.sum(exponent, axis=(2, 3))
    partial_value = jnp.einsum(
        "hqij,ijhd->qhd",
        exponent.astype(jnp.bfloat16),
        value_rows,
        preferred_element_type=jnp.float32,
    )
    return (partial_value, maximum, totals)


def cross_merge(first_part, second_part):
    part_first, max_first, total_first = first_part
    part_second, max_second, total_second = second_part
    overall = jnp.maximum(max_first, max_second)
    weight_first = jnp.exp(max_first - overall)
    weight_second = jnp.exp(max_second - overall)
    denominator = total_first * weight_first + total_second * weight_second
    mixed_out = (
        part_first * weight_first.T[:, :, None] + part_second * weight_second.T[:, :, None]
    ) / denominator.T[:, :, None]
    return (mixed_out, overall + jnp.log(denominator))


def cross_backward(
    queries,
    segment,
    text_kv,
    lengths,
    half_index,
    score_scale,
    grad_out,
    log_total,
    row_delta,
    maximum,
):
    item_count, token_span, doubled = text_kv.shape
    key_rows, value_rows = cross_split(text_kv, queries.shape[1], queries.shape[2])
    scores = cross_scores(queries, segment, key_rows, lengths, half_index, score_scale)
    prob_full = jnp.exp(scores - log_total[:, :, None, None])
    exponent_low = jnp.exp(scores - maximum[:, :, None, None]).astype(jnp.bfloat16)
    grad_prob = jnp.einsum(
        "qhd,ijhd->hqij", grad_out, value_rows, preferred_element_type=jnp.float32
    )
    grad_scores = (prob_full * (grad_prob - row_delta[:, :, None, None])).astype(jnp.bfloat16)
    grad_query = (
        jnp.einsum("hqij,ijhd->qhd", grad_scores, key_rows, preferred_element_type=jnp.float32)
        * score_scale
    )
    grad_keys = (
        jnp.einsum("hqij,qhd->ijhd", grad_scores, queries, preferred_element_type=jnp.float32)
        * score_scale
    )
    carried = grad_out.astype(jnp.float32) * jnp.exp(maximum - log_total).T[:, :, None]
    carried_high = carried.astype(jnp.bfloat16)
    carried_rest = (carried - carried_high.astype(jnp.float32)).astype(jnp.bfloat16)
    grad_values = jnp.einsum(
        "hqij,qhd->ijhd", exponent_low, carried_high, preferred_element_type=jnp.float32
    )
    grad_values = grad_values + jnp.einsum(
        "hqij,qhd->ijhd", exponent_low, carried_rest, preferred_element_type=jnp.float32
    )
    grad_kv = jnp.concatenate(
        [
            grad_keys.reshape(item_count, token_span, doubled // 2),
            grad_values.reshape(item_count, token_span, doubled // 2),
        ],
        axis=2,
    )
    return (grad_query, grad_kv)


def on_device(
    frames_in,
    frame_item,
    text_in,
    text_len,
    time_embed,
    cotangent,
    w_mod,
    b_mod,
    w_qkv,
    w_out,
    b_out,
    w_q_cross,
    w_kv_cross,
    w_out_cross,
    b_out_cross,
    w_up,
    b_up,
    w_down,
    b_down,
):
    text_side = lax.axis_index("text")
    partner_side = 1 - text_side
    row_count, width = frames_in.shape
    head_size = HEAD_DIM
    head_count = width // head_size
    score_scale = head_size ** (-0.5)
    item_count = time_embed.shape[0]
    segment = lax.dynamic_index_in_dim(frame_item, text_side, 0, keepdims=False)
    own_lengths = lax.dynamic_slice_in_dim(text_len, text_side * item_count, item_count)
    embedding = time_embed.astype(jnp.float32)
    condition = jax.nn.silu(embedding).astype(jnp.bfloat16)
    mod_items = rows_dot(condition, w_mod) + b_mod.astype(jnp.float32)
    onehot = (segment[:, None] == jnp.arange(item_count, dtype=jnp.int32)[None, :]).astype(
        jnp.float32
    )
    mod_rows = jnp.dot(onehot, mod_items, precision=highest)
    shift_a, scale_a, gate_a, shift_b, scale_b, shift_c, scale_c, gate_c = jnp.split(
        mod_rows, 8, axis=1
    )
    frames = frames_in.astype(jnp.float32)
    normed_a = modulate(frames, shift_a, scale_a).astype(jnp.bfloat16)
    packed = rows_dot(normed_a, w_qkv).astype(jnp.bfloat16)
    queries = packed[:, :width].reshape(row_count, head_count, head_size)
    key_rows = packed[:, width : 2 * width].reshape(row_count, head_count, head_size)
    value_rows = packed[:, 2 * width :].reshape(row_count, head_count, head_size)
    attended_full, self_log = self_forward(queries, key_rows, value_rows, segment, score_scale)
    attended = attended_full.astype(jnp.bfloat16)
    branch_a = rows_dot(attended, w_out) + b_out.astype(jnp.float32)
    after_a = frames + gate_a * branch_a
    normed_b = modulate(after_a, shift_b, scale_b).astype(jnp.bfloat16)
    cross_q = (
        rows_dot(normed_b, w_q_cross).astype(jnp.bfloat16).reshape(row_count, head_count, head_size)
    )
    text_kv = jnp.einsum(
        "itc,cf->itf", text_in, w_kv_cross, preferred_element_type=jnp.float32
    ).astype(jnp.bfloat16)
    own_kv = lax.dynamic_slice_in_dim(text_kv, text_side * item_count, item_count, 0)
    partner_kv = lax.dynamic_slice_in_dim(text_kv, partner_side * item_count, item_count, 0)
    fetched_kv = swapped(partner_kv, "text", 0)
    own_part = cross_forward(cross_q, segment, own_kv, own_lengths, text_side, score_scale)
    far_part = cross_forward(cross_q, segment, fetched_kv, own_lengths, partner_side, score_scale)
    mixed_out, cross_log = cross_merge(own_part, far_part)
    cross_out = mixed_out.reshape(row_count, width).astype(jnp.bfloat16)
    branch_b = rows_dot(cross_out, w_out_cross) + b_out_cross.astype(jnp.float32)
    after_b = after_a + branch_b
    normed_c = modulate(after_b, shift_c, scale_c).astype(jnp.bfloat16)
    hidden = rows_dot(normed_c, w_up) + b_up.astype(jnp.float32)
    active = gelu_tanh(hidden).astype(jnp.bfloat16)
    branch_c = rows_dot(active, w_down) + b_down.astype(jnp.float32)
    frames_out = after_b + gate_c * branch_c
    upstream = cotangent.astype(jnp.float32)
    grad_branch_c = gate_c * upstream
    grad_gate_c = upstream * branch_c
    low_branch_c = grad_branch_c.astype(jnp.bfloat16)
    grad_w_down = left_dot(active, low_branch_c)
    grad_b_down = jnp.sum(grad_branch_c, axis=0)
    grad_active = right_dot(low_branch_c, w_down)
    grad_hidden = jax.vjp(gelu_tanh, hidden)[1](grad_active)[0]
    low_hidden = grad_hidden.astype(jnp.bfloat16)
    grad_w_up = left_dot(normed_c, low_hidden)
    grad_b_up = jnp.sum(grad_hidden, axis=0)
    grad_after_b, grad_shift_c, grad_scale_c = jax.vjp(modulate, after_b, shift_c, scale_c)[1](
        right_dot(low_hidden, w_up)
    )
    grad_after_b = grad_after_b + upstream
    low_after_b = grad_after_b.astype(jnp.bfloat16)
    grad_w_out_cross = left_dot(cross_out, low_after_b)
    grad_b_out_cross = jnp.sum(grad_after_b, axis=0)
    grad_cross = (
        right_dot(low_after_b, w_out_cross)
        .astype(jnp.bfloat16)
        .reshape(row_count, head_count, head_size)
    )
    row_delta = jnp.sum(grad_cross.astype(jnp.float32) * mixed_out, axis=-1).T
    own_query, own_kv_grad = cross_backward(
        cross_q,
        segment,
        own_kv,
        own_lengths,
        text_side,
        score_scale,
        grad_cross,
        cross_log,
        row_delta,
        own_part[1],
    )
    far_query, far_kv_grad = cross_backward(
        cross_q,
        segment,
        fetched_kv,
        own_lengths,
        partner_side,
        score_scale,
        grad_cross,
        cross_log,
        row_delta,
        far_part[1],
    )
    grad_cross_q = own_query + far_query
    partner_kv_grad = swapped(far_kv_grad.astype(jnp.bfloat16), "text", 0).astype(far_kv_grad.dtype)
    grad_kv = jnp.where(
        text_side == 0,
        jnp.concatenate([own_kv_grad, partner_kv_grad], axis=0),
        jnp.concatenate([partner_kv_grad, own_kv_grad], axis=0),
    ).astype(jnp.bfloat16)
    text_grad = jnp.einsum("itf,cf->itc", grad_kv, w_kv_cross, preferred_element_type=jnp.float32)
    grad_w_kv_cross = jnp.einsum(
        "itc,itf->cf", text_in, grad_kv, preferred_element_type=jnp.float32
    )
    low_cross_q = grad_cross_q.reshape(row_count, width).astype(jnp.bfloat16)
    grad_w_q_cross = left_dot(normed_b, low_cross_q)
    grad_after_a, grad_shift_b, grad_scale_b = jax.vjp(modulate, after_a, shift_b, scale_b)[1](
        right_dot(low_cross_q, w_q_cross)
    )
    grad_after_a = grad_after_a + grad_after_b
    grad_branch_a = gate_a * grad_after_a
    grad_gate_a = grad_after_a * branch_a
    low_branch_a = grad_branch_a.astype(jnp.bfloat16)
    grad_w_out = left_dot(attended, low_branch_a)
    grad_b_out = jnp.sum(grad_branch_a, axis=0)
    grad_attended = (
        right_dot(low_branch_a, w_out)
        .astype(jnp.bfloat16)
        .reshape(row_count, head_count, head_size)
    )
    grad_queries, grad_keys, grad_values = self_backward(
        queries, key_rows, value_rows, segment, grad_attended, self_log, score_scale
    )
    grad_packed = jnp.concatenate(
        [
            grad_queries.reshape(row_count, width),
            grad_keys.reshape(row_count, width),
            grad_values.reshape(row_count, width),
        ],
        axis=1,
    ).astype(jnp.bfloat16)
    grad_w_qkv = left_dot(normed_a, grad_packed)
    grad_frames, grad_shift_a, grad_scale_a = jax.vjp(modulate, frames, shift_a, scale_a)[1](
        right_dot(grad_packed, w_qkv)
    )
    frames_grad = grad_frames + grad_after_a
    grad_mod_rows = jnp.concatenate(
        [
            grad_shift_a,
            grad_scale_a,
            grad_gate_a,
            grad_shift_b,
            grad_scale_b,
            grad_shift_c,
            grad_scale_c,
            grad_gate_c,
        ],
        axis=1,
    )
    grad_mod = lax.dot_general(onehot, grad_mod_rows, (((0,), (0,)), ((), ())), precision=highest)
    grad_b_mod = jnp.sum(grad_mod, axis=0)
    low_mod = grad_mod.astype(jnp.bfloat16)
    grad_w_mod = left_dot(condition, low_mod)
    time_grad = jax.vjp(jax.nn.silu, embedding)[1](right_dot(low_mod, w_mod))[0]
    shares = (
        lax.psum_scatter(grad_w_mod, "frames", scatter_dimension=0, tiled=True),
        lax.psum_scatter(grad_b_mod, "frames", scatter_dimension=0, tiled=True),
        lax.psum_scatter(grad_w_qkv, "frames", scatter_dimension=0, tiled=True),
        lax.psum_scatter(grad_w_out, "frames", scatter_dimension=0, tiled=True),
        lax.psum_scatter(grad_b_out, "frames", scatter_dimension=0, tiled=True),
        lax.psum_scatter(grad_w_q_cross, "frames", scatter_dimension=0, tiled=True),
        lax.psum_scatter(grad_w_kv_cross, "frames", scatter_dimension=0, tiled=True),
        lax.psum_scatter(grad_w_out_cross, "frames", scatter_dimension=0, tiled=True),
        lax.psum_scatter(grad_b_out_cross, "frames", scatter_dimension=0, tiled=True),
        lax.psum_scatter(grad_w_up, "frames", scatter_dimension=0, tiled=True),
        lax.psum_scatter(grad_b_up, "frames", scatter_dimension=0, tiled=True),
        lax.psum_scatter(grad_w_down, "frames", scatter_dimension=0, tiled=True),
        lax.psum_scatter(grad_b_down, "frames", scatter_dimension=0, tiled=True),
    )
    summed = (
        lax.psum(shares[0].astype(jnp.bfloat16), "text").astype(jnp.float32),
        lax.psum(shares[1].astype(jnp.bfloat16), "text").astype(jnp.float32),
        lax.psum(shares[2].astype(jnp.bfloat16), "text").astype(jnp.float32),
        lax.psum(shares[3].astype(jnp.bfloat16), "text").astype(jnp.float32),
        lax.psum(shares[4].astype(jnp.bfloat16), "text").astype(jnp.float32),
        lax.psum(shares[5].astype(jnp.bfloat16), "text").astype(jnp.float32),
        lax.psum(shares[6].astype(jnp.bfloat16), "text").astype(jnp.float32),
        lax.psum(shares[7].astype(jnp.bfloat16), "text").astype(jnp.float32),
        lax.psum(shares[8].astype(jnp.bfloat16), "text").astype(jnp.float32),
        lax.psum(shares[9].astype(jnp.bfloat16), "text").astype(jnp.float32),
        lax.psum(shares[10].astype(jnp.bfloat16), "text").astype(jnp.float32),
        lax.psum(shares[11].astype(jnp.bfloat16), "text").astype(jnp.float32),
        lax.psum(shares[12].astype(jnp.bfloat16), "text").astype(jnp.float32),
    )
    return (
        frames_out,
        frames_grad,
        text_grad,
        time_grad,
        summed[0],
        summed[1],
        summed[2],
        summed[3],
        summed[4],
        summed[5],
        summed[6],
        summed[7],
        summed[8],
        summed[9],
        summed[10],
        summed[11],
        summed[12],
    )


def solution(mesh):
    in_specs = (
        P(("frames", "text"), None),
        P("frames", None),
        P("frames", "text", None),
        P("frames"),
        P(("frames", "text"), None),
        P(("frames", "text"), None),
        P(),
        P(),
        P(),
        P(),
        P(),
        P(),
        P(),
        P(),
        P(),
        P(),
        P(),
        P(),
        P(),
    )
    out_specs = (
        P(("frames", "text"), None),
        P(("frames", "text"), None),
        P("frames", "text", None),
        P(("frames", "text"), None),
        P("frames", None),
        P("frames"),
        P("frames", None),
        P("frames", None),
        P("frames"),
        P("frames", None),
        P("frames", None),
        P("frames", None),
        P("frames"),
        P("frames", None),
        P("frames"),
        P("frames", None),
        P("frames"),
    )
    return jax.shard_map(
        on_device, mesh=mesh, in_specs=in_specs, out_specs=out_specs, check_vma=False
    )
```

profile of v0, /device:TPU:0, one launch (start us, length us, event | category | flops | bytes accessed | tf_op | source)
XLA Modules:
  0.0 1327.5 jit_solution(17480103630728655095)
XLA Ops:
  7.3 4.9 convolution_convert_fusion.1
  39.4 5.0 convolution_add_fusion
  44.4 10.2 fusion.153
  57.6 4.0 convolution_convert_fusion
  81.6 77.1 %while.27 = (s32[]{:T(128)}, bf16[2,512,12,64]{1,3,2,0:T(8,128)(2,1)}, f32[2,12,512]{2,1,0:T(8,128)}, bf16[2,512,12,64]{1,3,2,0:T(8,128)(2,1)}, bf16[1024,12,64]...) while((s32[]{:T(128)}, ...), condition=%wide.region_5.6_spmd, body=%wide.region_2.5_spmd.sunk | while | flops 1687152640 | bytes 196970704 | solution.py:79
  83.1 11.9 fusion.253
  95.0 11.9 fusion.254
  110.4 9.0 bitcast_dynamic-update-slice_fusion.6
  121.4 11.9 fusion.253
  133.3 11.9 fusion.254
  148.7 9.0 bitcast_dynamic-update-slice_fusion.6
  162.5 5.9 fusion.166
  176.8 10.8 fusion.32
  192.5 12.1 fusion.33
  204.6 26.6 %fusion.28 = (f32[12,1024]{1,0:T(8,128)S(1)}, bf16[12,1024,4,128]{1,3,2,0:T(8,128)(2,1)}, bf16[12,1024,4,128]{1,3,2,0:T(8,128)(2,1)}, f32[12,1024]{1,0:T(8,128)S(1)}) fusion(f32[12,1024,4,128]{1,3,2,0:T(8,128)} %get-tuple-element.368, f32[12,1024]{1,0:T(8,128)S(1)} %copy-done.50, f32[1024,4,128]{0,2,1:T(8,128)S(1)} %copy-done.19, ...), kind=kLoop, calls=%fused_computation.47 | loop fusion | flops 62889984 | bytes 79888384 | tf_op jit(solution)/shard_map/reduce_sum | solution.py:160
  234.9 8.9 fusion.45
  244.4 5.8 fusion.170
  255.3 4.1 fusion.67
  259.5 11.2 multiply_convert_fusion.3
  270.7 21.5 %fusion.173 = (f32[3072]{0:T(1024)}, bf16[1024,3072]{1,0:T(8,128)(2,1)}) fusion(bf16[3072,768]{1,0:T(8,128)(2,1)} %param.40, bf16[1024,768]{1,0:T(8,128)(2,1)S(1)} %copy-done.29, f32[1024,6144]{1,0:T(8,128)} %copy-done.5, f32[1024,3072]{1,0:T(8,128)} %get-tuple-element.378, f32[3072]{0:T(1024)S(1)} %copy-done.110), kind=kOutput, calls=%fused_computation.261 | convolution fusion | flops 4915983360 | bytes 28336128 | tf_op jit(solution)/shard_map/dot_general | solution.py:31
  292.2 9.6 multiply_reduce_fusion.2
  301.9 13.8 %fusion.165 = (f32[1024]{0:T(1024)S(1)}, f32[1024,768]{1,0:T(8,128)S(1)}, f32[1024,768]{1,0:T(8,128)}, f32[1024,768]{1,0:T(8,128)}) fusion(f32[1024]{0:T(1024)S(1)} %multiply_multiply_fusion.4, f32[1024,768]{1,0:T(8,128)S(1)} %copy-done.27, f32[1024]{0:T(1024)S(1)} %broadcast_multiply_fusion, f32[1024]{0:T(1024)S(1)} %fusion.147, ...), kind=kOutput, calls=%fused_computation.253 | convolution fusion | flops 4840487936 | bytes 33049600 | tf_op jit(solution)/shard_map/dot_general | solution.py:21
  320.4 4.3 convolution_convert_fusion.3
  327.1 19.1 %multiply_convert_fusion.1 = bf16[12,1024,4,128]{1,3,2,0:T(8,128)(2,1)} fusion(f32[12,1024,4,128]{1,3,2,0:T(8,128)} %get-tuple-element.370, f32[12,1024]{1,0:T(8,128)} %bitcast.341, f32[12,1024]{1,0:T(8,128)} %log_add_fusion.1, f32[1024,4,128]{0,2,1:T(8,128)} %get-tuple-element.362, bf16[1024,12,64,1]{0,2,3,1:T(8,128)(2,1)} %bitcast.301, ...), kind=kOutput, calls=%fused_computation.41 | convolution fusion | flops 843055104 | bytes 42303488 | tf_op jit(solution)/shard_map/qhd,ijhd->hqij/dot_general | solution.py:200
  346.3 19.1 %multiply_convert_fusion.2 = bf16[12,1024,4,128]{1,3,2,0:T(8,128)(2,1)} fusion(f32[12,1024,4,128]{1,3,2,0:T(8,128)} %get-tuple-element.368, f32[12,1024]{1,0:T(8,128)} %bitcast.342, f32[12,1024]{1,0:T(8,128)} %log_add_fusion.1, f32[1024,4,128]{0,2,1:T(8,128)} %copy-done.18, bf16[1024,12,64,1]{0,2,3,1:T(8,128)(2,1)} %bitcast.302, ...), kind=kOutput, calls=%fused_computation.42 | convolution fusion | flops 843055104 | bytes 42303488 | tf_op jit(solution)/shard_map/qhd,ijhd->hqij/dot_general | solution.py:200
  365.7 10.0 fusion.111
  378.5 6.3 fusion.41
  388.5 4.7 fusion.175
  393.2 10.5 fusion.95
  403.9 9.7 fusion.112
  416.6 4.0 multiply_reduce_fusion.1
  420.7 4.0 fusion.164
  433.4 7.5 fusion.92
  440.9 7.3 multiply_bitcast_fusion
  449.1 7.3 add_bitcast_fusion
  470.8 15.5 %convolution_bitcast_fusion = f32[768,1536]{0,1:T(8,128)} fusion(bf16[8,128,768]{2,1,0:T(8,128)(2,1)S(1)} %copy-done.119, bf16[4,128,1536]{1,2,0:T(8,128)(2,1)} %collective-permute-done.1, bf16[4,128,768]{1,2,0:T(8,128)(2,1)S(1)} %bitcast.339, bf16[4,128,768]{1,2,0:T(8,128)(2,1)S(1)} %bitcast.337, pred[]{:T(512)S(6)} %eq.50), kind=kOutput, calls=%fused_computation.93 | convolution fusion | flops 2436366336 | bytes 9437185 | tf_op jit(solution)/shard_map/itc,itf->cf/dot_general | solution.py:358
  486.2 6.1 copy.204
  493.8 180.0 %while.28 = (s32[]{:T(128)}, f32[1024,12,64]{0,2,1:T(8,128)}, f32[1024,12,64]{0,2,1:T(8,128)}, bf16[2,512,12,64]{1,3,2,0:T(8,128)(2,1)}, bf16[2,512,12,64]{1,3,2...) while((s32[]{:T(128)}, f32[1024,12,64]{0,2,1:T(8,128)}, ...), condition=%wide.region_21.22_spmd.clone, body=%wide.region_19.21_spmd.clone.sunk | while | flops 4126271488 | bytes 240421136 | solution.py:128
  495.4 12.4 fusion.264
  507.8 13.8 %bitcast_add_fusion.6 = f32[1024,12,64]{0,2,1:T(8,128)} fusion(f32[1024,12,64]{0,2,1:T(8,128)} %get-tuple-element.560, f32[12,512,1024]{2,1,0:T(8,128)} %fusion.264, f32[12,512]{1,0:T(8,128)S(1)} %dynamic-slice_bitcast_fusion.2, f32[512,1024]{1,0:T(8,128)S(1)} %compare_select_fusion.5, pred[]{:T(512)S(6)} %compare.3, ...), kind=kOutput, calls=%fused_computation.20.clone.1 | convolution fusion | flops 832045056 | bytes 34373636 | tf_op jit(solution)/shard_map/while/body/eval_jaxpr/hqk,qhd->khd/dot_general | solution.py:116
  521.6 18.9 %multiply_reduce_fusion.6 = (f32[12,512]{1,0:T(8,128)}, f32[12,512,1024]{2,1,0:T(8,128)}) fusion(f32[12,512,1024]{2,1,0:T(8,128)} %fusion.264, f32[12,512]{1,0:T(8,128)} %copy-done.32, f32[512,1024]{1,0:T(8,128)} %copy-done.2, bf16[1024,12,64]{0,2,1:T(8,128)(2,1)} %get-tuple-element.581, bf16[2,512,12,64]{1,3,2,0:T(8,128)(2,1)} %get-tuple-element.580, ...), kind=kOutput, calls=%fused_computation.16.clone.1 | convolution fusion | flops 836757504 | bytes 54845444 | tf_op jit(solution)/shard_map/while/body/eval_jaxpr/qhd,khd->hqk/dot_general | solution.py:100
  540.5 23.8 %multiply_convert_fusion.6 = bf16[12,512,1024]{2,1,0:T(8,128)(2,1)} fusion(f32[12,512,1024]{2,1,0:T(8,128)} %get-tuple-element.516, f32[12,512,1024]{2,1,0:T(8,128)} %fusion.264, f32[12,512]{1,0:T(8,128)} %get-tuple-element.517, f32[12,512]{1,0:T(8,128)} %copy-done.32, f32[512,1024]{1,0:T(8,128)} %copy-done.2), kind=kLoop, calls=%fused_computation.15.clone.1 | loop fusion | flops 37748736 | bytes 65060864 | tf_op jit(solution)/shard_map/while/body/eval_jaxpr/convert_element_type | solution.py:104
  564.3 9.8 bitcast_dynamic-update-slice_fusion.8
  574.1 9.6 bitcast_add_fusion.5
  585.2 12.4 fusion.264
  597.5 14.0 %bitcast_add_fusion.6 = f32[1024,12,64]{0,2,1:T(8,128)} fusion(f32[1024,12,64]{0,2,1:T(8,128)} %get-tuple-element.560, f32[12,512,1024]{2,1,0:T(8,128)} %fusion.264, f32[12,512]{1,0:T(8,128)S(1)} %dynamic-slice_bitcast_fusion.2, f32[512,1024]{1,0:T(8,128)S(1)} %compare_select_fusion.5, pred[]{:T(512)S(6)} %compare.3, ...), kind=kOutput, calls=%fused_computation.20.clone.1 | convolution fusion | flops 832045056 | bytes 34373636 | tf_op jit(solution)/shard_map/while/body/eval_jaxpr/hqk,qhd->khd/dot_general | solution.py:116
  611.5 18.6 %multiply_reduce_fusion.6 = (f32[12,512]{1,0:T(8,128)}, f32[12,512,1024]{2,1,0:T(8,128)}) fusion(f32[12,512,1024]{2,1,0:T(8,128)} %fusion.264, f32[12,512]{1,0:T(8,128)} %copy-done.32, f32[512,1024]{1,0:T(8,128)} %copy-done.2, bf16[1024,12,64]{0,2,1:T(8,128)(2,1)} %get-tuple-element.581, bf16[2,512,12,64]{1,3,2,0:T(8,128)(2,1)} %get-tuple-element.580, ...), kind=kOutput, calls=%fused_computation.16.clone.1 | convolution fusion | flops 836757504 | bytes 54845444 | tf_op jit(solution)/shard_map/while/body/eval_jaxpr/qhd,khd->hqk/dot_general | solution.py:100
  630.1 23.7 %multiply_convert_fusion.6 = bf16[12,512,1024]{2,1,0:T(8,128)(2,1)} fusion(f32[12,512,1024]{2,1,0:T(8,128)} %get-tuple-element.516, f32[12,512,1024]{2,1,0:T(8,128)} %fusion.264, f32[12,512]{1,0:T(8,128)} %get-tuple-element.517, f32[12,512]{1,0:T(8,128)} %copy-done.32, f32[512,1024]{1,0:T(8,128)} %copy-done.2), kind=kLoop, calls=%fused_computation.15.clone.1 | loop fusion | flops 37748736 | bytes 65060864 | tf_op jit(solution)/shard_map/while/body/eval_jaxpr/convert_element_type | solution.py:104
  653.8 9.8 bitcast_dynamic-update-slice_fusion.8
  663.7 9.8 bitcast_add_fusion.5
  681.9 9.3 fusion.85
  691.3 9.9 fusion.73
  701.3 11.5 fusion.154
  713.1 8.2 constant_dynamic-update-slice_fusion.2
  721.3 6.3 fusion.83
  751.2 12.9 fusion.172
  764.7 8.0 fusion.133
  783.6 113.7 %reduce-scatter.21.cloned.1.call-done = f32[48,3072]{1,0:T(8,128)} async-done(((f32[768,3072]{1,0:T(8,128)}), f32[48,3072]{1,0:T(8,128)}) %reduce-scatter.21.cloned.1.call-update) | async-done | bytes 589840 | tf_op jit(solution)/shard_map/reduce_scatter | solution.py:421
  899.1 113.4 %reduce-scatter.23.cloned.1.call-done = f32[192,768]{1,0:T(8,128)} async-done(((f32[3072,768]{1,0:T(8,128)}), f32[192,768]{1,0:T(8,128)}) %reduce-scatter.23.cloned.1.call-update) | async-done | bytes 589840 | tf_op jit(solution)/shard_map/reduce_scatter | solution.py:423
  1014.3 197.4 %reduce-scatter.11.cloned.1.call-done = f32[48,6144]{1,0:T(8,128)} async-done(((f32[768,6144]{1,0:T(8,128)}), f32[48,6144]{1,0:T(8,128)}) %reduce-scatter.11.cloned.1.call-update) | async-done | bytes 1179664 | tf_op jit(solution)/shard_map/reduce_scatter | solution.py:412
  1217.1 60.8 %all-reduce.5 = (bf16[6144]{0:T(1024)(128)(2,1)}, bf16[768]{0:T(1024)(128)(2,1)}, bf16[768]{0:T(1024)(128)(2,1)}, bf16[3072]{0:T(1024)(128)(2,1)}, bf16[768]{0:T(1024)(128)(2,1)}) all-reduce(f32[6144]{0:T(1024)} %get-tuple-element.384, f32[768]{0:T(1024)S(1)} %copy-done.108, ...), channel_id=3, replica_groups=mesh['frames'=16,'text'=2] {'frames'}, use_global_device_ids=true, to_apply=%region_27.28.clone | all-reduce | flops 11520 | bytes 69120
  1283.6 5.6 all-reduce.6
  1294.5 7.0 fusion.142
  1301.5 6.2 fusion.80
  (420 shorter events, 207.0 us)
Async XLA Ops:
  7.2 50.4 %copy-start = (bf16[768,2304]{1,0:T(8,128)(2,1)S(1)}, bf16[768,2304]{1,0:T(8,128)(2,1)}, u32[]{:S(2)}) copy-start(bf16[768,2304]{1,0:T(8,128)(2,1)} %param.31) | copy-start | bytes 10616836
  7.2 765.7 %reduce-scatter.19.cloned.1.call-start = ((), (), s32[]{:S(2)}) async-start(), calls=%async_computation.12 | async-start | bytes 2506752 | tf_op jit(solution)/shard_map/reduce_scatter | solution.py:419
  15.1 172.5 %collective-permute-start = (bf16[4,128,1536]{2,1,0:T(8,128)(2,1)}, bf16[4,128,1536]{2,1,0:T(8,128)(2,1)}, u32[]{:S(2)}, u32[]{:S(2)}) collective-permute-start(bf16[4,128,1536]{2,1,0:T(8,128)(2,1)} %constant_dynamic-slice_fusion.3), channel_id=1, source_target_pairs={{0,1},{1,0},{2,3},{3,2},{4,5},{5,4},{6,7},{7,6},{8,9},{9,8},{10,11... | collective-permute-start | bytes 4718600 | tf_op jit(solution)/shard_map/ppermute | solution.py:17
  22.5 32.1 %copy-start.79 = (f32[1024]{0:T(1024)}, f32[1024]{0:T(1024)S(1)}, u32[]{:S(2)}) copy-start(f32[1024]{0:T(1024)S(1)} %broadcast_multiply_fusion.2) | copy-start | bytes 12292
  24.6 30.1 %copy-start.87 = (f32[1024]{0:T(1024)}, f32[1024]{0:T(1024)S(1)}, u32[]{:S(2)}) copy-start(f32[1024]{0:T(1024)S(1)} %fusion.145) | copy-start | bytes 12292
  44.4 10.3 copy-start.12
  54.7 8.8 copy-start.5
  95.0 15.4 %copy-start.1 = (f32[12,512,1024]{2,1,0:T(8,128)S(1)}, f32[12,512,1024]{2,1,0:T(8,128)}, u32[]{:S(2)}) copy-start(f32[12,512,1024]{2,1,0:T(8,128)} %get-tuple-element.503) | copy-start | bytes 75497472 | tf_op jit(solution)/shard_map/while
  110.4 9.0 copy-start.75
  133.3 15.4 %copy-start.1 = (f32[12,512,1024]{2,1,0:T(8,128)S(1)}, f32[12,512,1024]{2,1,0:T(8,128)}, u32[]{:S(2)}) copy-start(f32[12,512,1024]{2,1,0:T(8,128)} %get-tuple-element.503) | copy-start | bytes 75497472 | tf_op jit(solution)/shard_map/while
  148.7 9.0 copy-start.75
  176.6 11.0 copy-start.23
  192.5 12.1 copy-start.19
  192.5 12.1 copy-start.20
  192.5 12.1 copy-start.50
  204.6 27.3 %copy-start.52 = (f32[12,1024]{1,0:T(8,128)}, f32[12,1024]{1,0:T(8,128)S(1)}, u32[]{:S(2)}) copy-start(f32[12,1024]{1,0:T(8,128)S(1)} %get-tuple-element.369) | copy-start | bytes 147460
  234.9 8.9 copy-start.7
  234.9 9.3 copy-start.49
  234.9 9.3 copy-start.77
  234.9 9.4 copy-start.94
  234.9 9.4 copy-start.95
  253.7 48.2 %copy-start.92 = (f32[1024]{0:T(1024)}, f32[1024]{0:T(1024)S(1)}, u32[]{:S(2)}) copy-start(f32[1024]{0:T(1024)S(1)} %broadcast_multiply_fusion) | copy-start | bytes 12292
  255.3 46.6 %copy-start.98 = (f32[1024]{0:T(1024)}, f32[1024]{0:T(1024)S(1)}, u32[]{:S(2)}) copy-start(f32[1024]{0:T(1024)S(1)} %fusion.147) | copy-start | bytes 12292
  259.5 11.2 copy-start.54
  259.5 11.2 copy-start.29
  270.7 21.5 %copy-start.27 = (f32[1024,768]{1,0:T(8,128)S(1)}, f32[1024,768]{1,0:T(8,128)}, u32[]{:S(2)}) copy-start(f32[1024,768]{1,0:T(8,128)} %copy-done.26) | copy-start | bytes 9437188
  292.2 9.7 copy-start.106
  301.8 13.9 %copy-start.34 = (f32[1024,768]{1,0:T(8,128)}, f32[1024,768]{1,0:T(8,128)S(1)}, u32[]{:S(2)}) copy-start(f32[1024,768]{1,0:T(8,128)S(1)} %get-tuple-element.376) | copy-start | bytes 9437188
  301.9 15.5 %copy-start.120 = (bf16[1024,12,64]{0,2,1:T(8,128)(2,1)S(1)}, bf16[1024,12,64]{0,2,1:T(8,128)(2,1)}, u32[]{:S(2)}) copy-start(bf16[1024,12,64]{0,2,1:T(8,128)(2,1)} %get-tuple-element.371) | copy-start | bytes 4718596
  315.8 109.0 %copy-start.100 = (f32[1024]{0:T(1024)}, f32[1024]{0:T(1024)S(1)}, u32[]{:S(2)}) copy-start(f32[1024]{0:T(1024)S(1)} %negate_multiply_fusion.2) | copy-start | bytes 12292
  365.4 409.1 %reduce-scatter.17.cloned.1.call-start = ((), (), s32[]{:S(2)}) async-start(), calls=%async_computation.11 | async-start | bytes 2506752 | tf_op jit(solution)/shard_map/reduce_scatter | solution.py:417
  365.6 12.2 copy-start.51
  365.6 12.2 copy-start.53
  365.6 12.2 copy-start.78
  365.7 12.8 copy-start.40
  365.7 19.2 %slice-start = ((s8[12582912]{0:T(1024)(128)(4,1)}), s8[4194304]{0:T(1024)(128)(4,1)S(1)}, s32[]{:S(2)}) async-start(s8[12582912]{0:T(1024)(128)(4,1)} %bitcast.298), calls=%async_computation.17 | async-start | bytes 8388608
  365.7 19.2 %slice-start.1 = ((s8[12582912]{0:T(1024)(128)(4,1)}), s8[4194304]{0:T(1024)(128)(4,1)S(1)}, s32[]{:S(2)}) async-start(s8[12582912]{0:T(1024)(128)(4,1)} %bitcast.298), calls=%async_computation.18 | async-start | bytes 8388608
  403.6 372.4 %reduce-scatter.15.cloned.1.call-start = ((), (), s32[]{:S(2)}) async-start(), calls=%async_computation.10 | async-start | bytes 2506752 | tf_op jit(solution)/shard_map/reduce_scatter | solution.py:415
  403.9 9.8 copy-start.48
  403.9 11.2 copy-start.67
  403.9 11.1 copy-start.82
  415.0 55.8 %collective-permute-start.1 = (bf16[4,128,1536]{1,2,0:T(8,128)(2,1)}, bf16[4,128,1536]{1,2,0:T(8,128)(2,1)}, u32[]{:S(2)}, u32[]{:S(2)}) collective-permute-start(bf16[4,128,1536]{1,2,0:T(8,128)(2,1)} %pad_maximum_fusion.3), channel_id=1, source_target_pairs={{0,1},{1,0},{2,3},{3,2},{4,5},{5,4},{6,7},{7,6},{8,9},{9,8},{10,11... | collective-permute-start | bytes 4718600 | tf_op jit(solution)/shard_map/ppermute | solution.py:17
  432.9 344.7 %reduce-scatter.25.cloned.1.call-start = ((), (), s32[]{:S(2)}) async-start(), calls=%async_computation.15 | async-start | bytes 5013504
  440.9 8.2 copy-start.16
  440.9 8.2 copy-start.72
  449.1 8.3 copy-start.57
  492.4 289.5 %reduce-scatter.13.cloned.1.call-start = ((), (), s32[]{:S(2)}) async-start(), calls=%async_computation.9 | async-start | bytes 7520256 | tf_op jit(solution)/shard_map/reduce_scatter | solution.py:414
  494.9 12.9 copy-start.32
  495.4 12.4 copy-start.2
  495.4 12.4 copy-start.17
  584.6 12.9 copy-start.32
  585.2 12.4 copy-start.2
  585.2 12.4 copy-start.17
  691.3 206.0 %reduce-scatter.21.cloned.1.call-start = ((), (), s32[]{:S(2)}) async-start(), calls=%async_computation.13 | async-start | bytes 10027008 | tf_op jit(solution)/shard_map/reduce_scatter | solution.py:421
  701.2 311.3 %reduce-scatter.23.cloned.1.call-start = ((), (), s32[]{:S(2)}) async-start(), calls=%async_computation.14 | async-start | bytes 10027008 | tf_op jit(solution)/shard_map/reduce_scatter | solution.py:423
  712.8 8.5 copy-start.80
  712.8 8.5 copy-start.101
  712.8 498.9 %reduce-scatter.11.cloned.1.call-start = ((), (), s32[]{:S(2)}) async-start(), calls=%async_computation.8 | async-start | bytes 20054016 | tf_op jit(solution)/shard_map/reduce_scatter | solution.py:412
  713.1 8.2 copy-start.14
  713.1 8.2 copy-start.25
  751.2 13.5 %copy-start.86 = (bf16[4,768]{1,0:T(4,128)(2,1)S(1)}, bf16[4,768]{1,0:T(4,128)(2,1)}, u32[]{:S(2)}) copy-start(bf16[4,768]{1,0:T(4,128)(2,1)} %param.27) | copy-start | bytes 18436
  772.7 535.1 %all-reduce.10.cloned.1.call-start = ((), (), s32[]{:S(2)}) async-start(), calls=%async_computation.16 | async-start | bytes 4030464 | tf_op jit(solution)/shard_map/psum | solution.py:433
  779.5 437.6 %copy-start.108 = (f32[768]{0:T(1024)S(1)}, f32[768]{0:T(1024)}, u32[]{:S(2)}) copy-start(f32[768]{0:T(1024)} %get-tuple-element.270) | copy-start | bytes 9220
  1309.6 10.1 copy-start.73
  (81 other events, 303.8 us)
Sparse Core Ops, SparseCore 0:
  365.5 63.3 reduce-scatter.18
  433.1 61.9 reduce-scatter.16
  498.9 61.8 reduce-scatter.14
  565.0 74.5 reduce-scatter.24
  691.4 90.4 reduce-scatter.12
  786.3 110.8 reduce-scatter.20
  901.3 111.1 reduce-scatter.22
  1017.2 194.5 reduce-scatter.10
  1215.8 61.5 all-reduce.9
where the time goes:
time: 1340 us; the launch traced here: 1330 us
  matrix products  511 us (38%)
  waiting for transfers between devices  427 us (32%)
  other arithmetic  186 us (14%)
  local copies, waits for them, and re-layouts  115 us (9%)
  blocking collectives  66.4 us (5%)
  between operations  17.3 us (1%)
    reduce_scatter x1, waiting for transfers between devices, on_device(): lax.psum_scatter(grad_w_mod, 'frames', scatter_dimension=0, tiled=True)  197 us
    reduce_scatter x1, waiting for transfers between devices, on_device(): lax.psum_scatter(grad_w_up, 'frames', scatter_dimension=0, tiled=True)  114 us
    reduce_scatter x1, waiting for transfers between devices, on_device(): lax.psum_scatter(grad_w_down, 'frames', scatter_dimension=0, tiled=True)  113 us
    unnamed x1, blocking collectives  60.8 us
    dot_general x7, matrix products, right_dot(): lax.dot_general(left_side, right_side, (((1,), (1,)), ((), ())), preferre...  58.5 us
    dot_general x7, matrix products, left_dot(): lax.dot_general(left_side, right_side, (((0,), (0,)), ((), ())), preferre...  49.2 us
    dot_general x4, matrix products, self_scores(): jnp.einsum('qhd,khd->hqk', query_rows, key_rows, preferred_element_type=j...  48.6 us
    convert_element_type x2, other arithmetic, one_block(): grad_scores = (prob_full * (grad_prob - row_delta)).astype(jnp.bfloat16)  47.5 us
  transfers between devices with their start and end apart: 11, of which 4 were waited for; matrix products, arithmetic and copies ran while one was open for 44% of the time, Pallas kernels for 0%

commit v1 on v0

v1 whole, which is shorter than its diff:
```python
import functools

import jax
import jax.numpy as jnp
from jax import lax
from jax.experimental import pallas as pl
from jax.experimental.pallas import tpu as pltpu
from jax.sharding import PartitionSpec as P

HEAD_DIM = 64
LANES = 128
VMEM_LIMIT = 56 << 20

epsilon = 1e-06
masked_add = -1000000000.0
highest = lax.Precision.HIGHEST
low_type = jnp.bfloat16


def rows_dot(left_side, right_side):
    return jnp.dot(left_side, right_side, preferred_element_type=jnp.float32)


def left_dot(left_side, right_side):
    return lax.dot_general(
        left_side, right_side, (((0,), (0,)), ((), ())), preferred_element_type=jnp.float32
    )


def right_dot(left_side, right_side):
    return lax.dot_general(
        left_side, right_side, (((1,), (1,)), ((), ())), preferred_element_type=jnp.float32
    )


def layer_norm(values):
    center = values - jnp.mean(values, axis=-1, keepdims=True)
    spread = jnp.mean(center * center, axis=-1, keepdims=True)
    return center * lax.rsqrt(spread + epsilon)


def modulate(values, shift_by, scale_by):
    return layer_norm(values) * (1.0 + scale_by) + shift_by


def gelu_tanh(inputs):
    return (
        0.5
        * inputs
        * (1.0 + jnp.tanh(0.7978845608028654 * (inputs + 0.044715 * inputs * inputs * inputs)))
    )


def head_lanes(value, head, scale=None):
    lane = lax.broadcasted_iota(jnp.int32, value.shape, 1)
    scaled = value if scale is None else value * jnp.asarray(scale, value.dtype)
    return jnp.where(lane // HEAD_DIM == head, scaled, jnp.zeros_like(scaled))


def fill_bias(code_column_ref, code_row_ref, bias_refs, key_split):
    half = code_row_ref.shape[1] // 2
    spans = ((0, key_split), (key_split, code_column_ref.shape[0]))
    for part, bias_ref in enumerate(bias_refs):
        if bias_ref is None:
            continue
        low, top = spans[part]
        bias_ref[...] = jnp.where(
            code_column_ref[low:top, :] == code_row_ref[:, part * half : (part + 1) * half],
            0.0,
            masked_add,
        )


def attend_kernel(
    q_ref, k_ref, v_ref, code_column_ref, code_row_ref, out_ref, log_ref, *bias_refs, key_split
):
    half = q_ref.shape[0] // 2
    scale = HEAD_DIM ** (-0.5)
    if len(bias_refs) == 1:
        bias_refs = (None,) + bias_refs

    @pl.when(pl.program_id(0) == 0)
    def _():
        fill_bias(code_column_ref, code_row_ref, bias_refs, key_split)

    value_t = v_ref[...].T
    key_spans = (slice(0, key_split), slice(key_split, k_ref.shape[0]))
    for part in range(2):
        rows = slice(part * half, (part + 1) * half)
        queries = q_ref[rows, :]
        keys = k_ref[key_spans[part], :]
        outs = []
        for head in range(2):
            scores = right_dot(keys, head_lanes(queries, head, scale))
            if bias_refs[part] is not None:
                scores = scores + bias_refs[part][...]
            peak = jnp.max(scores, axis=0, keepdims=True)
            exponent = jnp.exp(scores - peak)
            total = jnp.sum(exponent, axis=0, keepdims=True)
            outs.append(
                rows_dot(
                    value_t[HEAD_DIM * head : HEAD_DIM * (head + 1), key_spans[part]],
                    exponent.astype(low_type),
                )
                / total
            )
            log_ref[0, head : head + 1, rows] = peak + jnp.log(total)
        out_ref[rows, :] = jnp.concatenate(outs, axis=0).T.astype(low_type)


def attend_back_kernel(
    q_ref,
    k_ref,
    v_ref,
    grad_ref,
    log_ref,
    code_column_ref,
    code_row_ref,
    grad_q_ref,
    grad_k_ref,
    grad_v_ref,
    *bias_refs,
    key_split,
):
    half = q_ref.shape[0] // 2
    scale = HEAD_DIM ** (-0.5)
    if len(bias_refs) == 1:
        bias_refs = (None,) + bias_refs

    @pl.when(pl.program_id(0) == 0)
    def _():
        fill_bias(code_column_ref, code_row_ref, bias_refs, key_split)

    key_t = k_ref[...].T
    key_spans = (slice(0, key_split), slice(key_split, k_ref.shape[0]))
    for part in range(2):
        rows = slice(part * half, (part + 1) * half)
        queries = q_ref[rows, :]
        grads = grad_ref[rows, :]
        keys = k_ref[key_spans[part], :]
        values = v_ref[key_spans[part], :]
        grad_q, grad_k, grad_v = [], [], []
        for head in range(2):
            query_head = head_lanes(queries, head, scale)
            grad_head = head_lanes(grads, head)
            scores = right_dot(keys, query_head)
            if bias_refs[part] is not None:
                scores = scores + bias_refs[part][...]
            prob = jnp.exp(scores - log_ref[0, head : head + 1, rows])
            grad_prob = right_dot(values, grad_head)
            weighted = prob * grad_prob
            delta = jnp.sum(weighted, axis=0, keepdims=True)
            grad_scores = (weighted - prob * delta).astype(low_type)
            grad_k.append(rows_dot(grad_scores, query_head))
            grad_v.append(rows_dot(prob.astype(low_type), grad_head))
            grad_q.append(
                rows_dot(
                    key_t[HEAD_DIM * head : HEAD_DIM * (head + 1), key_spans[part]], grad_scores
                )
                * scale
            )
        grad_q_ref[rows, :] = jnp.concatenate(grad_q, axis=0).T.astype(low_type)
        grad_k_ref[key_spans[part], :] = (grad_k[0] + grad_k[1]).astype(low_type)
        grad_v_ref[key_spans[part], :] = (grad_v[0] + grad_v[1]).astype(low_type)


def attention_call(kernel, name, operands, columns, codes, log_total, outs, key_split, key_rows):
    rows = codes[1].shape[1]
    half = rows // 2
    pairs = operands[0].shape[1] // LANES if columns is None else columns[0]
    offsets = columns[1]
    in_specs = [
        pl.BlockSpec((array.shape[0], LANES), lambda step, offset=offset: (0, offset + step))
        for array, offset in zip(operands, offsets)
    ]
    extra = []
    log_spec = pl.BlockSpec((1, 8, rows), lambda step: (step, 0, 0))
    if log_total is not None:
        in_specs.append(log_spec)
        extra.append(log_total)
    in_specs += [
        pl.BlockSpec(codes[0].shape, lambda step: (0, 0)),
        pl.BlockSpec(codes[1].shape, lambda step: (0, 0)),
    ]
    out_shape, out_specs = [], []
    for count in outs:
        if count == "log":
            out_shape.append(jax.ShapeDtypeStruct((pairs, 8, rows), jnp.float32))
            out_specs.append(log_spec)
        else:
            out_shape.append(jax.ShapeDtypeStruct((count, pairs * LANES), low_type))
            out_specs.append(pl.BlockSpec((count, LANES), lambda step: (0, step)))
    scratch = [pltpu.VMEM((key_rows - key_split, half), jnp.float32)]
    if key_split != half:
        scratch = [pltpu.VMEM((key_split, half), jnp.float32)] + scratch
    products = 2 if log_total is None else 5
    cells = half * key_rows
    return pl.pallas_call(
        functools.partial(kernel, key_split=key_split),
        out_shape=out_shape,
        grid=(pairs,),
        in_specs=in_specs,
        out_specs=out_specs,
        scratch_shapes=scratch,
        compiler_params=pltpu.CompilerParams(vmem_limit_bytes=VMEM_LIMIT),
        cost_estimate=pl.CostEstimate(
            flops=products * pairs * 2 * cells * 256 * 2,
            transcendentals=pairs * 2 * cells,
            bytes_accessed=rows * pairs * LANES * 2 * 8,
        ),
        name=name,
    )(*operands, *extra, *codes)


def swapped(value, axis, stride):
    pairs = [(source, source ^ stride) for source in range(lax.axis_size(axis))]
    return lax.ppermute(value, axis, pairs)


def summed_low(kept, received):
    return (kept.astype(jnp.float32) + received.astype(jnp.float32)).astype(low_type)


def share_sum(grad, text_first):
    count = lax.axis_size("frames")
    bits = count.bit_length() - 1
    rows, columns = grad.shape
    spot = lax.axis_index("frames")
    value = grad.reshape((2,) * bits + (rows // count, columns))
    side = lax.axis_index("text")
    dims = list(range(bits))[::-1]
    split = columns // 2

    def along(value, bit):
        dim = dims.index(bit)
        mine = (spot >> bit) & 1
        kept = lax.dynamic_index_in_dim(value, mine, dim, keepdims=False)
        sent = lax.dynamic_index_in_dim(value, 1 - mine, dim, keepdims=False)
        dims.pop(dim)
        return summed_low(kept, swapped(sent, "frames", 1 << bit))

    value = along(value, 0)
    if text_first:
        kept = lax.dynamic_slice_in_dim(value, side * split, split, value.ndim - 1)
        sent = lax.dynamic_slice_in_dim(value, (1 - side) * split, split, value.ndim - 1)
        value = summed_low(kept, swapped(sent, "text", 1))
    for bit in range(1, bits):
        value = along(value, bit)
    if text_first:
        other = swapped(value, "text", 1)
        pair = jnp.where(
            side == 0,
            jnp.concatenate([value, other], axis=1),
            jnp.concatenate([other, value], axis=1),
        )
        return pair.astype(jnp.float32)
    return value.astype(jnp.float32) + swapped(value, "text", 1).astype(jnp.float32)


def gathered(value, order):
    count = lax.axis_size("frames")
    bits = count.bit_length() - 1
    spot = lax.axis_index("frames")
    side = lax.axis_index("text")
    shape = [1] * (bits + 1)
    value = value.reshape(tuple(shape) + value.shape)
    for step in order:
        if step == "text":
            dim, mine = bits, side
            other = swapped(value, "text", 1)
        else:
            dim, mine = bits - 1 - step, (spot >> step) & 1
            other = swapped(value, "frames", 1 << step)
        value = jnp.where(
            mine == 0,
            jnp.concatenate([value, other], axis=dim),
            jnp.concatenate([other, value], axis=dim),
        )
    return value.reshape((-1,) + value.shape[bits + 1 :][1:])


def on_device(
    frames_in,
    frame_item,
    text_in,
    text_len,
    time_embed,
    cotangent,
    w_mod,
    b_mod,
    w_qkv,
    w_out,
    b_out,
    w_q_cross,
    w_kv_cross,
    w_out_cross,
    b_out_cross,
    w_up,
    b_up,
    w_down,
    b_down,
):
    text_side = lax.axis_index("text")
    partner_side = 1 - text_side
    row_count, width = frames_in.shape
    half = row_count // 2
    item_count = time_embed.shape[0]
    token_span = text_in.shape[1]
    token_rows = item_count * 2 * token_span
    frame_bits = lax.axis_size("frames").bit_length() - 1
    segment = lax.dynamic_index_in_dim(frame_item, text_side, 0, keepdims=False)
    own_lengths = lax.dynamic_slice_in_dim(text_len, text_side * item_count, item_count)
    item_ids = jnp.arange(item_count, dtype=jnp.int32)

    own_text = lax.dynamic_slice_in_dim(text_in, text_side * item_count, item_count, 0)
    partner_text = lax.dynamic_slice_in_dim(text_in, partner_side * item_count, item_count, 0)
    fetched_text = swapped(partner_text, "text", 1)

    counts = jnp.sum((segment[None, :] == item_ids[:, None]).astype(jnp.int32), axis=1)
    big = jnp.argmax((counts == half).astype(jnp.int32)).astype(jnp.int32)
    start = jnp.sum((segment < big).astype(jnp.int32))
    segment = jnp.roll(jnp.mod(segment - big, item_count), -start)
    frames = jnp.roll(frames_in, -start, axis=0).astype(jnp.float32)
    upstream = jnp.roll(cotangent, -start, axis=0).astype(jnp.float32)
    lengths = jnp.roll(own_lengths, -big)
    embedding = jnp.roll(time_embed, -big, axis=0).astype(jnp.float32)
    text = jnp.roll(jnp.concatenate([own_text, fetched_text], axis=1), -big, axis=0)
    text = text.reshape(token_rows, text.shape[2])

    self_codes = (segment[:, None], segment[None, :])
    slot = jnp.arange(2 * token_span, dtype=jnp.int32)
    position = jnp.where(
        slot < token_span,
        text_side * token_span + slot,
        partner_side * token_span + slot - token_span,
    )
    token_code = jnp.where(position[None, :] < lengths[:, None], item_ids[:, None], -1)
    cross_codes = (token_code.reshape(token_rows, 1), segment[None, :])
    pairs = width // LANES

    condition = jax.nn.silu(embedding).astype(low_type)
    mod_items = rows_dot(condition, w_mod) + b_mod.astype(jnp.float32)
    onehot = (segment[:, None] == item_ids[None, :]).astype(jnp.float32)
    mod_rows = jnp.dot(onehot, mod_items, precision=highest)
    shift_a, scale_a, gate_a, shift_b, scale_b, shift_c, scale_c, gate_c = jnp.split(
        mod_rows, 8, axis=1
    )
    normed_a = modulate(frames, shift_a, scale_a).astype(low_type)
    packed = rows_dot(normed_a, w_qkv).astype(low_type)
    packed_columns = (pairs, (0, pairs, 2 * pairs, 0))
    attended, self_log = attention_call(
        attend_kernel,
        "self_forward",
        (packed, packed, packed),
        packed_columns,
        self_codes,
        None,
        (row_count, "log"),
        half,
        row_count,
    )
    branch_a = rows_dot(attended, w_out) + b_out.astype(jnp.float32)
    after_a = frames + gate_a * branch_a
    normed_b = modulate(after_a, shift_b, scale_b).astype(low_type)
    cross_q = rows_dot(normed_b, w_q_cross).astype(low_type)
    text_kv = rows_dot(text, w_kv_cross).astype(low_type)
    cross_columns = (pairs, (0, 0, pairs, 0))
    cross_out, cross_log = attention_call(
        attend_kernel,
        "cross_forward",
        (cross_q, text_kv, text_kv),
        cross_columns,
        cross_codes,
        None,
        (row_count, "log"),
        2 * token_span,
        token_rows,
    )
    branch_b = rows_dot(cross_out, w_out_cross) + b_out_cross.astype(jnp.float32)
    after_b = after_a + branch_b
    normed_c = modulate(after_b, shift_c, scale_c).astype(low_type)
    hidden = rows_dot(normed_c, w_up) + b_up.astype(jnp.float32)
    active = gelu_tanh(hidden).astype(low_type)
    branch_c = rows_dot(active, w_down) + b_down.astype(jnp.float32)
    frames_out = jnp.roll(after_b + gate_c * branch_c, start, axis=0)
    grad_branch_c = gate_c * upstream
    grad_gate_c = upstream * branch_c
    low_branch_c = grad_branch_c.astype(low_type)
    grad_w_down = left_dot(active, low_branch_c).astype(low_type)
    grad_b_down = jnp.sum(grad_branch_c, axis=0)
    grad_active = right_dot(low_branch_c, w_down)
    grad_hidden = jax.vjp(gelu_tanh, hidden)[1](grad_active)[0]
    low_hidden = grad_hidden.astype(low_type)
    grad_w_up = left_dot(normed_c, low_hidden).astype(low_type)
    grad_b_up = jnp.sum(grad_hidden, axis=0)
    sum_w_down = share_sum(grad_w_down, False)
    sum_w_up = share_sum(grad_w_up, True)
    grad_after_b, grad_shift_c, grad_scale_c = jax.vjp(modulate, after_b, shift_c, scale_c)[1](
        right_dot(low_hidden, w_up)
    )
    grad_after_b = grad_after_b + upstream
    low_after_b = grad_after_b.astype(low_type)
    grad_w_out_cross = left_dot(cross_out, low_after_b).astype(low_type)
    grad_b_out_cross = jnp.sum(grad_after_b, axis=0)
    grad_cross = right_dot(low_after_b, w_out_cross).astype(low_type)
    low_cross_q, grad_text_k, grad_text_v = attention_call(
        attend_back_kernel,
        "cross_backward",
        (cross_q, text_kv, text_kv, grad_cross),
        cross_columns,
        cross_codes,
        cross_log,
        (row_count, token_rows, token_rows),
        2 * token_span,
        token_rows,
    )
    text_sum = right_dot(grad_text_k, w_kv_cross[:, :width]) + right_dot(
        grad_text_v, w_kv_cross[:, width:]
    )
    text_sum = jnp.roll(text_sum.reshape(item_count, 2 * token_span, -1), big, axis=0)
    own_text_grad = text_sum[:, :token_span]
    sent_text_grad = text_sum[:, token_span:].astype(low_type)
    partner_text_grad = swapped(sent_text_grad, "text", 1).astype(jnp.float32)
    text_grad = jnp.where(
        text_side == 0,
        jnp.concatenate([own_text_grad, partner_text_grad], axis=0),
        jnp.concatenate([partner_text_grad, own_text_grad], axis=0),
    )
    grad_w_kv_cross = jnp.concatenate(
        [left_dot(text, grad_text_k).astype(low_type), left_dot(text, grad_text_v).astype(low_type)],
        axis=1,
    )
    grad_w_q_cross = left_dot(normed_b, low_cross_q).astype(low_type)
    cross_sum = share_sum(
        jnp.concatenate([grad_w_kv_cross, grad_w_q_cross, grad_w_out_cross], axis=1), True
    )
    grad_after_a, grad_shift_b, grad_scale_b = jax.vjp(modulate, after_a, shift_b, scale_b)[1](
        right_dot(low_cross_q, w_q_cross)
    )
    grad_after_a = grad_after_a + grad_after_b
    grad_branch_a = gate_a * grad_after_a
    grad_gate_a = grad_after_a * branch_a
    low_branch_a = grad_branch_a.astype(low_type)
    grad_w_out = left_dot(attended, low_branch_a).astype(low_type)
    grad_b_out = jnp.sum(grad_branch_a, axis=0)
    grad_attended = right_dot(low_branch_a, w_out).astype(low_type)
    grad_packed = attention_call(
        attend_back_kernel,
        "self_backward",
        (packed, packed, packed, grad_attended),
        packed_columns,
        self_codes,
        self_log,
        (row_count, row_count, row_count),
        half,
        row_count,
    )
    grad_w_qkv = [left_dot(normed_a, piece).astype(low_type) for piece in grad_packed]
    self_sum = share_sum(jnp.concatenate(grad_w_qkv + [grad_w_out], axis=1), False)
    grad_normed_a = sum(
        right_dot(piece, w_qkv[:, index * width : (index + 1) * width])
        for index, piece in enumerate(grad_packed)
    )
    grad_frames, grad_shift_a, grad_scale_a = jax.vjp(modulate, frames, shift_a, scale_a)[1](
        grad_normed_a
    )
    frames_grad = jnp.roll(grad_frames + grad_after_a, start, axis=0)
    grad_mod_rows = jnp.concatenate(
        [
            grad_shift_a,
            grad_scale_a,
            grad_gate_a,
            grad_shift_b,
            grad_scale_b,
            grad_shift_c,
            grad_scale_c,
            grad_gate_c,
        ],
        axis=1,
    )
    grad_mod = lax.dot_general(onehot, grad_mod_rows, (((0,), (0,)), ((), ())), precision=highest)
    low_mod = grad_mod.astype(low_type)
    time_grad = jax.vjp(jax.nn.silu, embedding)[1](right_dot(low_mod, w_mod))[0]
    time_grad = jnp.roll(time_grad, big, axis=0)

    order = tuple(range(frame_bits - 1, 0, -1)) + ("text", 0)
    all_mod = gathered(jnp.roll(low_mod, big, axis=0), order)
    all_conditions = gathered(jnp.roll(condition, big, axis=0), order)
    share = lax.axis_size("frames")
    spot = lax.axis_index("frames")
    own_conditions = lax.dynamic_slice_in_dim(
        all_conditions, spot * (width // share), width // share, 1
    )
    grad_w_mod = left_dot(own_conditions, all_mod)
    mod_columns = all_mod.shape[1] // share
    grad_b_mod = jnp.sum(
        lax.dynamic_slice_in_dim(all_mod, spot * mod_columns, mod_columns, 1).astype(jnp.float32),
        axis=0,
    )
    biases = [grad_b_out, grad_b_out_cross, grad_b_up, grad_b_down]
    bias_sum = lax.psum(
        lax.psum_scatter(
            jnp.concatenate([bias.reshape(share, -1) for bias in biases], axis=1),
            "frames",
            scatter_dimension=0,
            tiled=True,
        ),
        "text",
    )[0]
    bias_cuts, done = [], 0
    for bias in biases:
        bias_cuts.append(bias_sum[done : done + bias.shape[0] // share])
        done += bias.shape[0] // share
    sum_kv_cross = cross_sum[:, : 2 * width]
    sum_q_cross = cross_sum[:, 2 * width : 3 * width]
    sum_out_cross = cross_sum[:, 3 * width :]
    return (
        frames_out,
        frames_grad,
        text_grad,
        time_grad,
        grad_w_mod,
        grad_b_mod,
        self_sum[:, : 3 * width],
        self_sum[:, 3 * width :],
        bias_cuts[0],
        sum_q_cross,
        sum_kv_cross,
        sum_out_cross,
        bias_cuts[1],
        sum_w_up,
        bias_cuts[2],
        sum_w_down,
        bias_cuts[3],
    )


def solution(mesh):
    in_specs = (
        P(("frames", "text"), None),
        P("frames", None),
        P("frames", "text", None),
        P("frames"),
        P(("frames", "text"), None),
        P(("frames", "text"), None),
    ) + (P(),) * 13
    out_specs = (
        P(("frames", "text"), None),
        P(("frames", "text"), None),
        P("frames", "text", None),
        P(("frames", "text"), None),
        P("frames", None),
        P("frames"),
        P("frames", None),
        P("frames", None),
        P("frames"),
        P("frames", None),
        P("frames", None),
        P("frames", None),
        P("frames"),
        P("frames", None),
        P("frames"),
        P("frames", None),
        P("frames"),
    )
    return jax.shard_map(
        on_device, mesh=mesh, in_specs=in_specs, out_specs=out_specs, check_vma=False
    )
```

time: 1340 us -> 653 us (0.49)
  matrix products: 511 us -> 177 us
  waiting for transfers between devices: 427 us -> 111 us
  Pallas kernels: 0 us -> 82.3 us
  other arithmetic: 186 us -> 111 us
  local copies, waits for them, and re-layouts: 115 us -> 57.1 us
  starting transfers between devices: 4.56 us -> 33 us
    reduce_scatter x7 -> x0, waiting for transfers between devices: 427 us -> none  [the longest x1 197 us: on_device(): lax.psum_scatter(grad_w_mod, 'frames', scatter_dimension=0, tiled=True)]
    dot_general x31 -> x0, matrix products: 335 us -> none  [the longest x4 48.6 us: self_scores(): jnp.einsum('qhd,khd->hqk', query_rows, key_rows, preferred_element_type=j...]
    ppermute x2 -> x34, waiting for transfers between devices: 0.01 us -> 111 us  [swapped(): return lax.ppermute(value, axis, pairs)]
    pallas_call x0 -> x4, Pallas kernels: none -> 82.3 us  [attention_call(): pl.pallas_call(functools.partial(kernel, key_split=key_split), out_shape=...]
    convert_element_type x25 -> x26, other arithmetic: 89.1 us -> 31.1 us  [the longest x18 12.5 us: summed_low(): (kept.astype(jnp.float32) + received.astype(jnp.float32)).astype(low_type)]
    reduce_sum x5 -> x3, other arithmetic: 57.8 us -> 8.64 us  [the longest x1 6.86 us: on_device(): grad_b_out = jnp.sum(grad_branch_a, axis=0)]
    ppermute x2 -> x34, starting transfers between devices: 3.01 us -> 33 us  [swapped(): return lax.ppermute(value, axis, pairs)]
    unnamed x250 -> x192, local copies, waits for them, and re-layouts: 45 us -> 15.2 us
  transfers between devices with their start and end apart: 11 -> 34, of which waited for: 4 -> 16; matrix products, arithmetic and copies ran while one was open for 44% -> 21% of each run, Pallas kernels for 0% -> 2%
where the time goes in v1:
time: 653 us; the launch traced here: 643 us
  matrix products  177 us (27%)
  other arithmetic  111 us (17%)
  waiting for transfers between devices  111 us (17%)
  Pallas kernels  82.3 us (13%)
  blocking collectives  64.4 us (10%)
  local copies, waits for them, and re-layouts  57.1 us (9%)
  starting transfers between devices  33 us (5%)
  between operations  7.6 us (1%)
    ppermute x34, waiting for transfers between devices, swapped(): return lax.ppermute(value, axis, pairs)  111 us
    pallas_call x4, Pallas kernels, attention_call(): pl.pallas_call(functools.partial(kernel, key_split=key_split), out_shape=...  82.3 us
    unnamed x1, blocking collectives  59.5 us
    dot_general x11, matrix products, right_dot(): lax.dot_general(left_side, right_side, (((1,), (1,)), ((), ())), preferre...  57.5 us
    dot_general x8, matrix products, rows_dot(): return jnp.dot(left_side, right_side, preferred_element_type=jnp.float32)  49.5 us
    dot_general x11, matrix products, left_dot(): lax.dot_general(left_side, right_side, (((0,), (0,)), ((), ())), preferre...  43.6 us
    ppermute x34, starting transfers between devices, swapped(): return lax.ppermute(value, axis, pairs)  33 us
    unnamed x192, local copies, waits for them, and re-layouts  15.2 us
  transfers between devices with their start and end apart: 34, of which 16 were waited for; matrix products, arithmetic and copies ran while one was open for 21% of the time, Pallas kernels for 2%

profile of v1, /device:TPU:0, one launch (start us, length us, event | category | flops | bytes accessed | tf_op | source)
XLA Modules:
  0.0 643.2 jit_solution(11775323412464147608)
XLA Ops:
  3.2 2.9 collective-permute-start
  10.2 2.6 collective-permute-start.2
  20.5 5.0 convolution_add_fusion
  25.5 13.3 %fusion.61 = f32[1024,6144]{1,0:T(8,128)} fusion(f32[4,6144]{1,0:T(4,128)S(1)} %convolution_add_fusion, s32[1024]{0:T(1024)S(1)} %fusion.84), kind=kOutput, calls=%fused_computation.162 | convolution fusion | flops 301993984 | bytes 25268224 | tf_op jit(solution)/shard_map/dot_general | solution.py:344
  39.9 3.5 fusion.16
  43.8 5.4 convolution_convert_fusion.1.q_ref.k_ref.v_ref
  49.2 15.8 %self_forward.1 = (bf16[1024,768]{1,0:T(8,128)(2,1)}, f32[6,8,1024]{2,1,0:T(8,128)}) custom-call(bf16[1024,2304]{1,0:T(8,128)(2,1)} %convolution_convert_fusion.1.q_ref.k_ref.v_ref, bf16[1024,2304]{1,0:T(8,128)(2,1)} %convolution_convert_fusion.1.q_ref.k_ref.v_ref, bf16[1024,2304]{1,0:T(8,128)(2,1)} %convolution_convert_fusion.1.q_ref.k_ref.v_ref, ...), custom_call_target="tpu_custom_call" | custom-call | flops 6442450944 | bytes 12582912 | tf_op jit(solution)/shard_map/self_forward/pallas_call | solution.py:198
  65.0 5.5 fusion.107
  71.1 4.3 fusion.25
  95.6 3.5 collective-permute-done.5
  99.2 3.8 fusion.36
  103.9 3.0 fusion.38
  106.9 4.0 convolution_convert_fusion.4.k_ref.v_ref
  110.9 16.9 %cross_forward.1 = (bf16[1024,768]{1,0:T(8,128)(2,1)}, f32[6,8,1024]{2,1,0:T(8,128)}) custom-call(bf16[1024,768]{1,0:T(8,128)(2,1)} %convolution_convert_fusion.7.q_ref, bf16[1024,1536]{1,0:T(8,128)(2,1)} %convolution_convert_fusion.4.k_ref.v_ref, bf16[1024,1536]{1,0:T(8,128)(2,1)} %convolution_convert_fusion.4.k_ref.v_ref, s32[1024,1]{1,0:T(8,128)} %bitcast.223, ...), custom_call_target="tpu_custom_call" | custom-call | flops 6442450944 | bytes 12582912 | tf_op jit(solution)/shard_map/cross_forward/pallas_call | solution.py:198
  127.8 2.9 fusion.110
  131.4 4.8 fusion.24
  136.2 11.3 %multiply_convert_fusion = (bf16[1024,3072]{1,0:T(8,128)(2,1)}, f32[1024,3072]{1,0:T(8,128)}) fusion(f32[3072]{0:T(1024)S(1)} %copy-done.60, bf16[1024,768]{1,0:T(8,128)(2,1)S(1)} %fusion.24, bf16[768,3072]{1,0:T(8,128)(2,1)S(1)} %bitcast.239), kind=kOutput, calls=%fused_computation.9 | convolution fusion | flops 4863295488 | bytes 25178112 | tf_op jit(solution)/shard_map/dot_general | solution.py:21
  147.5 21.6 %fusion.111 = (f32[3072]{0:T(1024)}, bf16[1024,3072]{1,0:T(8,128)(2,1)}) fusion(bf16[3072,768]{1,0:T(8,128)(2,1)} %param.42, bf16[1024,768]{1,0:T(8,128)(2,1)} %fusion.36, f32[1024,6144]{1,0:T(8,128)} %fusion.61, f32[1024,3072]{1,0:T(8,128)} %get-tuple-element.92, f32[3072]{0:T(1024)S(1)} %copy-done.60), kind=kOutput, calls=%fused_computation.289 | convolution fusion | flops 4915983360 | bytes 28336128 | tf_op jit(solution)/shard_map/dot_general | solution.py:31
  169.1 9.8 %convolution_convert_fusion.3 = bf16[768,3072]{1,0:T(8,128)(2,1)} fusion(bf16[1024,768]{1,0:T(8,128)(2,1)S(1)} %fusion.24, bf16[1024,3072]{1,0:T(8,128)(2,1)} %get-tuple-element.99), kind=kOutput, calls=%fused_computation.20 | convolution fusion | flops 4834197504 | bytes 12582912 | tf_op jit(solution)/shard_map/dot_general | solution.py:25
  178.9 8.9 %multiply_reduce_fusion.1 = (f32[1024]{0:T(1024)S(1)}, f32[1024,768]{1,0:T(8,128)S(1)}) fusion(f32[1024,768]{1,0:T(8,128)S(1)} %get-tuple-element.88, f32[1024]{0:T(1024)S(1)} %broadcast_multiply_fusion, f32[1024,6144]{1,0:T(8,128)} %fusion.61, bf16[768,3072]{1,0:T(8,128)(2,1)} %param.40, bf16[1024,3072]{1,0:T(8,128)(2,1)S(1)} %copy-done.67), kind=kOutput, calls=%fused_computation.79 | convolution fusion | flops 4835769344 | bytes 20455424 | tf_op jit(solution)/shard_map/dot_general | solution.py:31
  187.9 10.8 %convolution_convert_fusion.2 = bf16[3072,768]{1,0:T(8,128)(2,1)} fusion(bf16[1024,3072]{1,0:T(8,128)(2,1)} %get-tuple-element.91, bf16[1024,768]{1,0:T(8,128)(2,1)S(1)} %copy-done.29, f32[1024,6144]{1,0:T(8,128)} %fusion.61), kind=kOutput, calls=%fused_computation.19 | convolution fusion | flops 4836556800 | bytes 15728640 | tf_op jit(solution)/shard_map/dot_general | solution.py:25
  198.8 12.9 %fusion.106 = (f32[1024]{0:T(1024)S(1)}, f32[1024,768]{1,0:T(8,128)S(1)}, f32[1024,768]{1,0:T(8,128)}, f32[1024,768]{1,0:T(8,128)}) fusion(f32[1024]{0:T(1024)S(1)} %multiply_multiply_fusion.4, f32[1024,768]{1,0:T(8,128)S(1)} %get-tuple-element.88, f32[1024]{0:T(1024)S(1)} %broadcast_multiply_fusion, f32[1024]{0:T(1024)S(1)} %fusion.87, ...), kind=kOutput, calls=%fused_computation.285 | convolution fusion | flops 4840487936 | bytes 33049600 | tf_op jit(solution)/shard_map/dot_general | solution.py:21
  211.7 2.9 convolution_convert_fusion.8
  214.6 2.8 convolution_convert_fusion.6.grad_ref
  217.4 25.0 %cross_backward.1 = (bf16[1024,768]{1,0:T(8,128)(2,1)}, bf16[1024,768]{1,0:T(8,128)(2,1)}, bf16[1024,768]{1,0:T(8,128)(2,1)}) custom-call(bf16[1024,768]{1,0:T(8,128)(2,1)} %convolution_convert_fusion.7.q_ref, bf16[1024,1536]{1,0:T(8,128)(2,1)} %convolution_convert_fusion.4.k_ref.v_ref, bf16[1024,1536]{1,0:T(8,128)(2,1)} %convolution_convert_fusion.4.k_ref.v_ref, ...), custom_call_target="tpu_custom_call" | custom-call | flops 16106127360 | bytes 12582912 | tf_op jit(solution)/shard_map/cross_backward/pallas_call | solution.py:198
  242.5 4.1 convolution_convert_fusion.9
  246.6 3.7 multiply_reduce_fusion
  250.3 4.1 fusion.105
  254.7 4.9 fusion.42
  259.6 2.6 convolution_convert_fusion.5.grad_ref
  264.7 24.5 %self_backward.1 = (bf16[1024,768]{1,0:T(8,128)(2,1)}, bf16[1024,768]{1,0:T(8,128)(2,1)}, bf16[1024,768]{1,0:T(8,128)(2,1)}) custom-call(bf16[1024,2304]{1,0:T(8,128)(2,1)} %convolution_convert_fusion.1.q_ref.k_ref.v_ref, bf16[1024,2304]{1,0:T(8,128)(2,1)} %convolution_convert_fusion.1.q_ref.k_ref.v_ref, ...), custom_call_target="tpu_custom_call" | custom-call | flops 16106127360 | bytes 12582912 | tf_op jit(solution)/shard_map/self_backward/pallas_call | solution.py:198
  289.2 3.3 fusion.51
  295.1 2.8 fusion.53
  303.0 5.8 constant_dynamic-update-slice_fusion.2
  308.9 6.9 %fusion.41 = (f32[768]{0:T(1024)}, f32[1024]{0:T(1024)S(1)}, f32[768]{0:T(1024)S(1)}, f32[768]{0:T(1024)}) fusion(f32[1024,768]{1,0:T(8,128)} %get-tuple-element.49, f32[1024,6144]{1,0:T(8,128)S(1)} %bitcast.199, f32[1024,768]{1,0:T(8,128)} %get-tuple-element.97, f32[1024]{0:T(1024)S(1)} %copy-done.47, bf16[1024,768]{1,0:T(8,128)(2,1)} %copy-done.4, ...), kind=kLoop, calls=%fused_computation.124 | loop fusion | flops 13366016 | bytes 22041604 | tf_op jit(solution)/shard_map/reduce_sum | solution.py:445
  315.8 4.6 fusion.104
  324.4 5.4 multiply_dynamic-update-slice_fusion.2
  341.3 4.1 fusion.20
  345.4 12.9 %convolution_convert_fusion = bf16[4,6144]{1,0:T(4,128)(2,1)S(1)} fusion(f32[1024,6144]{1,0:T(8,128)} %fusion.20, s32[1024]{0:T(1024)S(1)} %copy-done.42), kind=kOutput, calls=%fused_computation.11 | convolution fusion | flops 302018560 | bytes 25219072 | tf_op jit(solution)/shard_map/dot_general | solution.py:481
  359.1 3.2 fusion.78
  380.4 6.6 %copy.129 = bf16[768,3072]{1,0:T(8,128)(2,1)} copy(bf16[768,3072]{0,1:T(8,128)(2,1)} %pad_maximum_fusion.1) | data formatting | bytes 9437184 | tf_op jit(solution)/shard_map/concatenate | solution.py:435
  387.0 3.3 dynamic-slice_bitcast_fusion
  395.1 59.5 %all-reduce = f32[16,336]{1,0:T(8,128)} all-reduce(f32[16,336]{1,0:T(8,128)} %pad_maximum_fusion.2), channel_id=2, replica_groups=mesh['frames'=16,'text'=2] {'frames'}, use_global_device_ids=true, to_apply=%region_20.24.clone | all-reduce | flops 5376 | bytes 43008
  455.9 4.9 psum.7
  461.5 5.2 pad_maximum_fusion
  466.7 6.7 %copy.128 = bf16[768,3072]{1,0:T(8,128)(2,1)} copy(bf16[768,3072]{0,1:T(8,128)(2,1)} %pad_maximum_fusion) | data formatting | bytes 9437184 | tf_op jit(solution)/shard_map/concatenate | solution.py:459
  474.6 7.6 %fusion.22 = (f32[1024,768]{1,0:T(8,128)}, f32[1024,768]{1,0:T(8,128)}) fusion(s32[]{:T(128)S(6)} %select_n.597, f32[1024,768]{1,0:T(8,128)} %get-tuple-element.64, f32[1024,768]{1,0:T(8,128)} %get-tuple-element.58), kind=kLoop, calls=%fused_computation.54 | loop fusion | flops 1572864 | bytes 12582916 | tf_op jit(solution)/shard_map/jit(_roll_dynamic)/concatenate | solution.py:467
  482.4 4.5 collective-permute-done.8
  487.4 5.5 collective-permute-done.9
  495.0 6.1 collective-permute-done.10
  508.6 3.8 select_n.571
  514.2 2.9 fusion.70
  519.5 2.7 fusion.10
  523.9 2.6 fusion.11
  527.6 2.6 fusion.12
  532.3 15.9 %collective-permute-done.30 = bf16[2,2,192,768]{3,2,0,1:T(8,128)(2,1)S(1)} collective-permute-done((bf16[2,2,192,768]{3,2,0,1:T(8,128)(2,1)S(1)}, bf16[2,2,192,768]{3,2,0,1:T(8,128)(2,1)S(1)}, u32[]{:S(2)}, u32[]{:S(2)}) %collective-permute-start.30) | collective-permute-done | bytes 1179680 | tf_op jit(solution)/shard_map/ppermute | solution.py:217
  553.7 22.1 %collective-permute-done.18 = bf16[2,2,2,48,1536]{4,3,2,1,0:T(8,128)(2,1)S(1)} collective-permute-done((bf16[2,2,2,48,1536]{4,3,2,1,0:T(8,128)(2,1)S(1)}, bf16[2,2,2,48,1536]{4,3,2,1,0:T(8,128)(2,1)S(1)}, u32[]{:S(2)}, u32[]{:S(2)}) %collective-permute-start.18) | collective-permute-done | bytes 1179680 | tf_op jit(solution)/shard_map/ppermute | solution.py:217
  578.8 3.0 collective-permute-start.32
  581.8 4.4 collective-permute-done.25
  586.5 11.7 %collective-permute-done.19 = bf16[2,2,48,1536]{3,2,1,0:T(8,128)(2,1)S(1)} collective-permute-done((bf16[2,2,48,1536]{3,2,1,0:T(8,128)(2,1)S(1)}, bf16[2,2,48,1536]{3,2,1,0:T(8,128)(2,1)S(1)}, u32[]{:S(2)}, u32[]{:S(2)}) %collective-permute-start.19) | collective-permute-done | bytes 589856 | tf_op jit(solution)/shard_map/ppermute | solution.py:217
  603.6 9.7 %collective-permute-done.26 = bf16[2,48,1536]{2,1,0:T(8,128)(2,1)S(1)} collective-permute-done((bf16[2,48,1536]{2,1,0:T(8,128)(2,1)S(1)}, bf16[2,48,1536]{2,1,0:T(8,128)(2,1)S(1)}, u32[]{:S(2)}, u32[]{:S(2)}) %collective-permute-start.26) | collective-permute-done | bytes 294944 | tf_op jit(solution)/shard_map/ppermute | solution.py:217
  614.4 4.8 collective-permute-done.20
  621.1 10.7 %collective-permute-done.21 = bf16[48,1536]{1,0:T(8,128)(2,1)S(1)} collective-permute-done((bf16[48,1536]{1,0:T(8,128)(2,1)S(1)}, bf16[48,1536]{1,0:T(8,128)(2,1)S(1)}, u32[]{:S(2)}, u32[]{:S(2)}) %collective-permute-start.21) | collective-permute-done | bytes 147488 | tf_op jit(solution)/shard_map/ppermute | solution.py:217
  634.1 4.0 collective-permute-done.22
  (377 shorter events, 128.4 us)
Async XLA Ops:
  0.7 64.4 %copy-start = (bf16[768,768]{1,0:T(8,128)(2,1)S(1)}, bf16[768,768]{1,0:T(8,128)(2,1)}, u32[]{:S(2)}) copy-start(bf16[768,768]{1,0:T(8,128)(2,1)} %param.34) | copy-start | bytes 3538948
  0.7 8.8 %copy-start.56 = (bf16[4,768]{1,0:T(4,128)(2,1)S(1)}, bf16[4,768]{1,0:T(4,128)(2,1)}, u32[]{:S(2)}) copy-start(bf16[4,768]{1,0:T(4,128)(2,1)} %param.29) | copy-start | bytes 18436
  0.7 14.7 %copy-start.61 = (bf16[6144]{0:T(1024)(128)(2,1)S(1)}, bf16[6144]{0:T(1024)(128)(2,1)}, u32[]{:S(2)}) copy-start(bf16[6144]{0:T(1024)(128)(2,1)} %param.32) | copy-start | bytes 36868
  3.2 100.8 %collective-permute-start = (bf16[4,128,768]{2,1,0:T(8,128)(2,1)}, bf16[4,128,768]{2,1,0:T(8,128)(2,1)}, u32[]{:S(2)}, u32[]{:S(2)}) collective-permute-start(bf16[4,128,768]{2,1,0:T(8,128)(2,1)} %get-tuple-element.65), channel_id=1, source_target_pairs={{0,1},{1,0},{2,3},{3,2},{4,5},{5,4},{6,7},{7,6},{8,9},{9,8},{10,11... | collective-permute-start | bytes 2359304 | tf_op jit(solution)/shard_map/ppermute | solution.py:217
  10.2 76.2 %collective-permute-start.2 = (bf16[1,1,1,1,1,4,768]{6,5,4,3,2,1,0:T(4,128)(2,1)}, bf16[1,1,1,1,1,4,768]{6,5,4,3,2,1,0:T(4,128)(2,1)}, u32[]{:S(2)}, u32[]{:S(2)}) collective-permute-start(bf16[1,1,1,1,1,4,768]{6,5,4,3,2,1,0:T(4,128)(2,1)} %get-tuple-element.80), channel_id=1, source_target_pairs={{0,16},{2,18},{4,20},{6,22},{8,24},{10,26},{12,28},{14,30},{16,0},... | collective-permute-start | bytes 18440 | tf_op jit(solution)/shard_map/ppermute | solution.py:217
  16.1 22.8 %copy-start.41 = (s32[1024]{0:T(1024)}, s32[1024]{0:T(1024)S(1)}, u32[]{:S(2)}) copy-start(s32[1024]{0:T(1024)S(1)} %fusion.84) | copy-start | bytes 12292
  18.6 46.4 %copy-start.4 = (bf16[1024,768]{1,0:T(8,128)(2,1)}, bf16[1024,768]{1,0:T(8,128)(2,1)S(1)}, u32[]{:S(2)}) copy-start(bf16[1024,768]{1,0:T(8,128)(2,1)S(1)} %get-tuple-element.57) | copy-start | bytes 4718596
  18.7 21.2 %copy-start.46 = (f32[1024]{0:T(1024)}, f32[1024]{0:T(1024)S(1)}, u32[]{:S(2)}) copy-start(f32[1024]{0:T(1024)S(1)} %broadcast_multiply_fusion.2) | copy-start | bytes 12292
  25.5 14.4 %copy-start.63 = (bf16[768]{0:T(1024)(128)(2,1)S(1)}, bf16[768]{0:T(1024)(128)(2,1)}, u32[]{:S(2)}) copy-start(bf16[768]{0:T(1024)(128)(2,1)} %param.35) | copy-start | bytes 4612
  25.5 14.4 %copy-start.49 = (f32[1024]{0:T(1024)S(1)}, f32[1024]{0:T(1024)}, u32[]{:S(2)}) copy-start(f32[1024]{0:T(1024)} %fusion.85) | copy-start | bytes 12292
  39.9 25.2 %copy-start.52 = (f32[768]{0:T(1024)}, f32[768]{0:T(1024)S(1)}, u32[]{:S(2)}) copy-start(f32[768]{0:T(1024)S(1)} %convert_element_type.353) | copy-start | bytes 9220
  75.6 23.6 %copy-start.12 = (bf16[1024,768]{1,0:T(8,128)(2,1)S(1)}, bf16[1024,768]{1,0:T(8,128)(2,1)}, u32[]{:S(2)}) copy-start(bf16[1024,768]{1,0:T(8,128)(2,1)} %param.30) | copy-start | bytes 4718596
  87.2 3.8 collective-permute-start.3
  91.0 3.9 collective-permute-start.4
  94.9 4.2 collective-permute-start.5
  99.2 3.9 collective-permute-start.6
  110.9 17.0 %copy-start.3 = (f32[1024,768]{1,0:T(8,128)S(1)}, f32[1024,768]{1,0:T(8,128)}, u32[]{:S(2)}) copy-start(f32[1024,768]{1,0:T(8,128)} %copy-done.2) | copy-start | bytes 9437188
  110.9 17.0 %copy-start.62 = (f32[768]{0:T(1024)S(1)}, f32[768]{0:T(1024)}, u32[]{:S(2)}) copy-start(f32[768]{0:T(1024)} %convert_element_type.357) | copy-start | bytes 9220
  110.9 17.0 %copy-start.65 = (bf16[768,768]{1,0:T(8,128)(2,1)S(1)}, bf16[768,768]{1,0:T(8,128)(2,1)}, u32[]{:S(2)}) copy-start(bf16[768,768]{1,0:T(8,128)(2,1)} %param.38) | copy-start | bytes 3538948
  130.8 68.0 %copy-start.10 = (f32[1024,768]{1,0:T(8,128)}, f32[1024,768]{1,0:T(8,128)S(1)}, u32[]{:S(2)}) copy-start(f32[1024,768]{1,0:T(8,128)S(1)} %get-tuple-element.88) | copy-start | bytes 9437188
  169.1 9.8 %copy-start.67 = (bf16[1024,3072]{1,0:T(8,128)(2,1)S(1)}, bf16[1024,3072]{1,0:T(8,128)(2,1)}, u32[]{:S(2)}) copy-start(bf16[1024,3072]{1,0:T(8,128)(2,1)} %get-tuple-element.99) | copy-start | bytes 18874372
  178.9 8.9 %copy-start.29 = (bf16[1024,768]{1,0:T(8,128)(2,1)S(1)}, bf16[1024,768]{1,0:T(8,128)(2,1)}, u32[]{:S(2)}) copy-start(bf16[1024,768]{1,0:T(8,128)(2,1)} %fusion.36) | copy-start | bytes 4718596
  187.9 10.9 %copy-start.18 = (f32[1024,768]{1,0:T(8,128)}, f32[1024,768]{1,0:T(8,128)S(1)}, u32[]{:S(2)}) copy-start(f32[1024,768]{1,0:T(8,128)S(1)} %get-tuple-element.90) | copy-start | bytes 9437188
  198.8 12.9 %copy-start.71 = (bf16[1024,768]{1,0:T(8,128)(2,1)S(1)}, bf16[1024,768]{1,0:T(8,128)(2,1)}, u32[]{:S(2)}) copy-start(bf16[1024,768]{1,0:T(8,128)(2,1)} %get-tuple-element.33) | copy-start | bytes 4718596
  217.4 25.0 %copy-start.25 = (bf16[1024,768]{1,0:T(8,128)(2,1)S(1)}, bf16[1024,768]{1,0:T(8,128)(2,1)}, u32[]{:S(2)}) copy-start(bf16[1024,768]{1,0:T(8,128)(2,1)} %copy-done.24) | copy-start | bytes 4718596
  295.1 13.7 %slice-start = ((s8[25165824]{0:T(1024)(128)(4,1)}), s8[4194304]{0:T(1024)(128)(4,1)S(1)}, s32[]{:S(2)}) async-start(s8[25165824]{0:T(1024)(128)(4,1)} %bitcast.198), calls=%async_computation | async-start | bytes 8388608
  295.1 13.7 %slice-start.1 = ((s8[25165824]{0:T(1024)(128)(4,1)}), s8[4194304]{0:T(1024)(128)(4,1)S(1)}, s32[]{:S(2)}) async-start(s8[25165824]{0:T(1024)(128)(4,1)} %bitcast.198), calls=%async_computation.1 | async-start | bytes 8388608
  298.0 10.9 %slice-start.2 = ((s8[25165824]{0:T(1024)(128)(4,1)}), s8[4194304]{0:T(1024)(128)(4,1)S(1)}, s32[]{:S(2)}) async-start(s8[25165824]{0:T(1024)(128)(4,1)} %bitcast.198), calls=%async_computation.2 | async-start | bytes 8388608
  341.3 17.8 %slice-start.6 = ((s8[9437184]{0:T(1024)(128)(4,1)}), s8[4194304]{0:T(1024)(128)(4,1)S(1)}, s32[]{:S(2)}) async-start(s8[9437184]{0:T(1024)(128)(4,1)} %bitcast.200), calls=%async_computation.6 | async-start | bytes 8388608
  345.3 13.7 %slice-start.7 = ((s8[9437184]{0:T(1024)(128)(4,1)}), s8[4194304]{0:T(1024)(128)(4,1)S(1)}, s32[]{:S(2)}) async-start(s8[9437184]{0:T(1024)(128)(4,1)} %bitcast.200), calls=%async_computation.7 | async-start | bytes 8388608
  345.3 13.7 %slice-start.8 = ((s8[9437184]{0:T(1024)(128)(4,1)}), s8[1048576]{0:T(1024)(128)(4,1)S(1)}, s32[]{:S(2)}) async-start(s8[9437184]{0:T(1024)(128)(4,1)} %bitcast.200), calls=%async_computation.8 | async-start | bytes 2097152
  345.3 13.7 %copy-start.57 = (bf16[4,768]{1,0:T(4,128)(2,1)S(1)}, bf16[4,768]{1,0:T(4,128)(2,1)}, u32[]{:S(2)}) copy-start(bf16[4,768]{1,0:T(4,128)(2,1)} %param.29) | copy-start | bytes 18436
  374.5 142.6 %collective-permute-start.29 = (bf16[2,2,2,192,768]{4,3,0,1,2:T(8,128)(2,1)}, bf16[2,2,2,192,768]{4,3,0,1,2:T(8,128)(2,1)}, u32[]{:S(2)}, u32[]{:S(2)}) collective-permute-start(bf16[2,2,2,192,768]{4,3,0,1,2:T(8,128)(2,1)} %bitcast.196), channel_id=1, source_target_pairs={{0,2},{2,0},{4,6},{6,4},{8,10},{10,8},{12,14},{14,12},{16,18},{18,... | collective-permute-start | bytes 7077896 | tf_op jit(solution)/shard_map/ppermute | solution.py:217
  377.0 142.5 %collective-permute-start.23 = (bf16[2,2,2,48,3072]{4,3,0,1,2:T(8,128)(2,1)}, bf16[2,2,2,48,3072]{4,3,0,1,2:T(8,128)(2,1)}, u32[]{:S(2)}, u32[]{:S(2)}) collective-permute-start(bf16[2,2,2,48,3072]{4,3,0,1,2:T(8,128)(2,1)} %bitcast.197), channel_id=1, source_target_pairs={{0,2},{2,0},{4,6},{6,4},{8,10},{10,8},{12,14},{14,12},{16,18},{18,... | collective-permute-start | bytes 7077896 | tf_op jit(solution)/shard_map/ppermute | solution.py:217
  387.0 74.5 %copy-start.35 = (bf16[768,768]{0,1:T(8,128)(2,1)S(1)}, bf16[768,768]{0,1:T(8,128)(2,1)}, u32[]{:S(2)}) copy-start(bf16[768,768]{0,1:T(8,128)(2,1)} %convolution_convert_fusion.12) | copy-start | bytes 3538948
  390.4 133.6 %collective-permute-start.17 = (bf16[2,2,2,48,3072]{4,3,2,1,0:T(8,128)(2,1)}, bf16[2,2,2,48,3072]{4,3,2,1,0:T(8,128)(2,1)}, u32[]{:S(2)}, u32[]{:S(2)}) collective-permute-start(bf16[2,2,2,48,3072]{4,3,2,1,0:T(8,128)(2,1)} %dynamic-slice_bitcast_fusion), channel_id=1, source_target_pairs={{0,2},{2,0},{4,6},{6,4},{8,10},{10,8},{12,14},{14,12},{16,18},{18,... | collective-permute-start | bytes 7077896 | tf_op jit(solution)/shard_map/ppermute | solution.py:217
  473.4 8.7 %collective-permute-start.7 = (bf16[1,1,1,1,1,4,6144]{6,5,4,3,2,1,0:T(4,128)(2,1)S(1)}, bf16[1,1,1,1,1,4,6144]{6,5,4,3,2,1,0:T(4,128)(2,1)S(1)}, u32[]{:S(2)}, u32[]{:S(2)}) collective-permute-start(bf16[1,1,1,1,1,4,6144]{6,5,4,3,2,1,0:T(4,128)(2,1)S(1)} %copy-done.45), channel_id=1, source_target_pairs={{0,16},{2,18},{4,20},{6,22},{8,24},{10,26},{12,28},{14,30},{16,0},... | collective-permute-start | bytes 147464 | tf_op jit(solution)/shard_map/ppermute | solution.py:217
  474.1 29.9 %collective-permute-start.1 = (bf16[4,128,768]{2,1,0:T(8,128)(2,1)}, bf16[4,128,768]{2,1,0:T(8,128)(2,1)S(1)}, u32[]{:S(2)}, u32[]{:S(2)}) collective-permute-start(bf16[4,128,768]{2,1,0:T(8,128)(2,1)} %slice.106), channel_id=1, source_target_pairs={{0,1},{1,0},{2,3},{3,2},{4,5},{5,4},{6,7},{7,6},{8,9},{9,8},{10,11... | collective-permute-start | bytes 2359304 | tf_op jit(solution)/shard_map/ppermute | solution.py:217
  474.6 27.7 %slice-start.11 = ((s8[4718592]{0:T(1024)(128)(4,1)}), s8[4194304]{0:T(1024)(128)(4,1)S(1)}, s32[]{:S(2)}) async-start(s8[4718592]{0:T(1024)(128)(4,1)} %bitcast.206), calls=%async_computation.11 | async-start | bytes 8388608
  474.6 27.7 %slice-start.12 = ((s8[4718592]{0:T(1024)(128)(4,1)}), s8[524288]{0:T(1024)(128)(4,1)S(1)}, s32[]{:S(2)}) async-start(s8[4718592]{0:T(1024)(128)(4,1)} %bitcast.206), calls=%async_computation.12 | async-start | bytes 1048576
  482.3 4.7 collective-permute-start.8
  487.2 5.7 collective-permute-start.9
  493.2 7.8 %collective-permute-start.10 = (bf16[2,2,2,1,1,4,6144]{6,5,4,3,2,1,0:T(4,128)(2,1)S(1)}, bf16[2,2,2,1,1,4,6144]{6,5,4,3,2,1,0:T(4,128)(2,1)S(1)}, u32[]{:S(2)}, u32[]{:S(2)}) collective-permute-start(bf16[2,2,2,1,1,4,6144]{6,5,4,3,2,1,0:T(4,128)(2,1)S(1)} %maximum_select_fusion.4), channel_id=1, source_target_pairs={{0,1},{1,0},{2,3},{3,2},{4,5},{5,4},{6,7},{7,6},{8,9},{9,8},{10,11... | collective-permute-start | bytes 1179656 | tf_op jit(solution)/shard_map/ppermute | solution.py:217
  501.6 4.9 collective-permute-start.11
  504.0 23.6 %collective-permute-start.12 = (bf16[2,2,2,48,3072]{4,3,2,1,0:T(8,128)(2,1)}, bf16[2,2,2,48,3072]{4,3,2,1,0:T(8,128)(2,1)}, u32[]{:S(2)}, u32[]{:S(2)}) collective-permute-start(bf16[2,2,2,48,3072]{4,3,2,1,0:T(8,128)(2,1)} %dynamic-slice_bitcast_fusion.1), channel_id=1, source_target_pairs={{0,2},{2,0},{4,6},{6,4},{8,10},{10,8},{12,14},{14,12},{16,18},{18,... | collective-permute-start | bytes 7077896 | tf_op jit(solution)/shard_map/ppermute | solution.py:217
  519.4 28.9 %collective-permute-start.30 = (bf16[2,2,192,768]{3,2,0,1:T(8,128)(2,1)S(1)}, bf16[2,2,192,768]{3,2,0,1:T(8,128)(2,1)S(1)}, u32[]{:S(2)}, u32[]{:S(2)}) collective-permute-start(bf16[2,2,192,768]{3,2,0,1:T(8,128)(2,1)S(1)} %dynamic-slice_bitcast_fusion.2), channel_id=1, source_target_pairs={{0,4},{2,6},{4,0},{6,2},{8,12},{10,14},{12,8},{14,10},{16,20},{18,... | collective-permute-start | bytes 3538952 | tf_op jit(solution)/shard_map/ppermute | solution.py:217
  522.4 28.9 %collective-permute-start.24 = (bf16[2,2,2,48,1536]{4,3,0,1,2:T(8,128)(2,1)S(1)}, bf16[2,2,2,48,1536]{4,3,0,1,2:T(8,128)(2,1)S(1)}, u32[]{:S(2)}, u32[]{:S(2)}) collective-permute-start(bf16[2,2,2,48,1536]{4,3,0,1,2:T(8,128)(2,1)S(1)} %constant_dynamic-slice_fusion.4), channel_id=1, source_target_pairs={{0,1},{1,0},{2,3},{3,2},{4,5},{5,4},{6,7},{7,6},{8,9},{9,8},{10,11... | collective-permute-start | bytes 3538952 | tf_op jit(solution)/shard_map/ppermute | solution.py:217
  526.7 49.2 %collective-permute-start.18 = (bf16[2,2,2,48,1536]{4,3,2,1,0:T(8,128)(2,1)S(1)}, bf16[2,2,2,48,1536]{4,3,2,1,0:T(8,128)(2,1)S(1)}, u32[]{:S(2)}, u32[]{:S(2)}) collective-permute-start(bf16[2,2,2,48,1536]{4,3,2,1,0:T(8,128)(2,1)S(1)} %constant_dynamic-slice_fusion.7), channel_id=1, source_target_pairs={{0,1},{1,0},{2,3},{3,2},{4,5},{5,4},{6,7},{7,6},{8,9},{9,8},{10,11... | collective-permute-start | bytes 3538952 | tf_op jit(solution)/shard_map/ppermute | solution.py:217
  530.3 47.8 %collective-permute-start.13 = (bf16[2,2,48,3072]{3,2,1,0:T(8,128)(2,1)S(1)}, bf16[2,2,48,3072]{3,2,1,0:T(8,128)(2,1)S(1)}, u32[]{:S(2)}, u32[]{:S(2)}) collective-permute-start(bf16[2,2,48,3072]{3,2,1,0:T(8,128)(2,1)S(1)} %dynamic-slice_bitcast_fusion.3), channel_id=1, source_target_pairs={{0,4},{2,6},{4,0},{6,2},{8,12},{10,14},{12,8},{14,10},{16,20},{18,... | collective-permute-start | bytes 3538952 | tf_op jit(solution)/shard_map/ppermute | solution.py:217
  548.6 30.0 %collective-permute-start.31 = (bf16[2,192,768]{2,1,0:T(8,128)(2,1)S(1)}, bf16[2,192,768]{2,1,0:T(8,128)(2,1)S(1)}, u32[]{:S(2)}, u32[]{:S(2)}) collective-permute-start(bf16[2,192,768]{2,1,0:T(8,128)(2,1)S(1)} %dynamic-slice_bitcast_fusion.4), channel_id=1, source_target_pairs={{0,8},{2,10},{4,12},{6,14},{8,0},{10,2},{12,4},{14,6},{16,24},{18,... | collective-permute-start | bytes 1769480 | tf_op jit(solution)/shard_map/ppermute | solution.py:217
  551.6 34.6 %collective-permute-start.25 = (bf16[2,2,48,1536]{3,2,0,1:T(8,128)(2,1)S(1)}, bf16[2,2,48,1536]{3,2,0,1:T(8,128)(2,1)S(1)}, u32[]{:S(2)}, u32[]{:S(2)}) collective-permute-start(bf16[2,2,48,1536]{3,2,0,1:T(8,128)(2,1)S(1)} %dynamic-slice_bitcast_fusion.5), channel_id=1, source_target_pairs={{0,4},{2,6},{4,0},{6,2},{8,12},{10,14},{12,8},{14,10},{16,20},{18,... | collective-permute-start | bytes 1769480 | tf_op jit(solution)/shard_map/ppermute | solution.py:217
  576.3 21.9 %collective-permute-start.19 = (bf16[2,2,48,1536]{3,2,1,0:T(8,128)(2,1)S(1)}, bf16[2,2,48,1536]{3,2,1,0:T(8,128)(2,1)S(1)}, u32[]{:S(2)}, u32[]{:S(2)}) collective-permute-start(bf16[2,2,48,1536]{3,2,1,0:T(8,128)(2,1)S(1)} %dynamic-slice_bitcast_fusion.6), channel_id=1, source_target_pairs={{0,4},{2,6},{4,0},{6,2},{8,12},{10,14},{12,8},{14,10},{16,20},{18,... | collective-permute-start | bytes 1769480 | tf_op jit(solution)/shard_map/ppermute | solution.py:217
  578.5 22.1 %collective-permute-start.14 = (bf16[2,48,3072]{2,1,0:T(8,128)(2,1)S(1)}, bf16[2,48,3072]{2,1,0:T(8,128)(2,1)S(1)}, u32[]{:S(2)}, u32[]{:S(2)}) collective-permute-start(bf16[2,48,3072]{2,1,0:T(8,128)(2,1)S(1)} %dynamic-slice_bitcast_fusion.7), channel_id=1, source_target_pairs={{0,8},{2,10},{4,12},{6,14},{8,0},{10,2},{12,4},{14,6},{16,24},{18,... | collective-permute-start | bytes 1769480 | tf_op jit(solution)/shard_map/ppermute | solution.py:217
  578.8 23.1 %collective-permute-start.32 = (bf16[192,768]{1,0:T(8,128)(2,1)S(1)}, bf16[192,768]{1,0:T(8,128)(2,1)S(1)}, u32[]{:S(2)}, u32[]{:S(2)}) collective-permute-start(bf16[192,768]{1,0:T(8,128)(2,1)S(1)} %dynamic-slice_bitcast_fusion.8), channel_id=1, source_target_pairs={{0,16},{2,18},{4,20},{6,22},{8,24},{10,26},{12,28},{14,30},{16,0},... | collective-permute-start | bytes 884744 | tf_op jit(solution)/shard_map/ppermute | solution.py:217
  586.4 26.9 %collective-permute-start.26 = (bf16[2,48,1536]{2,1,0:T(8,128)(2,1)S(1)}, bf16[2,48,1536]{2,1,0:T(8,128)(2,1)S(1)}, u32[]{:S(2)}, u32[]{:S(2)}) collective-permute-start(bf16[2,48,1536]{2,1,0:T(8,128)(2,1)S(1)} %dynamic-slice_bitcast_fusion.9), channel_id=1, source_target_pairs={{0,8},{2,10},{4,12},{6,14},{8,0},{10,2},{12,4},{14,6},{16,24},{18,... | collective-permute-start | bytes 884744 | tf_op jit(solution)/shard_map/ppermute | solution.py:217
  598.4 20.9 %collective-permute-start.20 = (bf16[2,48,1536]{2,1,0:T(8,128)(2,1)S(1)}, bf16[2,48,1536]{2,1,0:T(8,128)(2,1)S(1)}, u32[]{:S(2)}, u32[]{:S(2)}) collective-permute-start(bf16[2,48,1536]{2,1,0:T(8,128)(2,1)S(1)} %dynamic-slice_bitcast_fusion.10), channel_id=1, source_target_pairs={{0,8},{2,10},{4,12},{6,14},{8,0},{10,2},{12,4},{14,6},{16,24},{18,... | collective-permute-start | bytes 884744 | tf_op jit(solution)/shard_map/ppermute | solution.py:217
  600.8 18.6 %collective-permute-start.15 = (bf16[48,3072]{1,0:T(8,128)(2,1)S(1)}, bf16[48,3072]{1,0:T(8,128)(2,1)S(1)}, u32[]{:S(2)}, u32[]{:S(2)}) collective-permute-start(bf16[48,3072]{1,0:T(8,128)(2,1)S(1)} %dynamic-slice_bitcast_fusion.11), channel_id=1, source_target_pairs={{0,16},{2,18},{4,20},{6,22},{8,24},{10,26},{12,28},{14,30},{16,0},... | collective-permute-start | bytes 884744 | tf_op jit(solution)/shard_map/ppermute | solution.py:217
  601.9 40.1 %collective-permute-start.33 = (bf16[192,768]{1,0:T(8,128)(2,1)S(1)}, bf16[192,768]{1,0:T(8,128)(2,1)S(1)}, u32[]{:S(2)}, u32[]{:S(2)}) collective-permute-start(bf16[192,768]{1,0:T(8,128)(2,1)S(1)} %fusion.57), channel_id=1, source_target_pairs={{0,1},{1,0},{2,3},{3,2},{4,5},{5,4},{6,7},{7,6},{8,9},{9,8},{10,11... | collective-permute-start | bytes 884744 | tf_op jit(solution)/shard_map/ppermute | solution.py:217
  613.4 20.1 %collective-permute-start.27 = (bf16[48,1536]{1,0:T(8,128)(2,1)S(1)}, bf16[48,1536]{1,0:T(8,128)(2,1)S(1)}, u32[]{:S(2)}, u32[]{:S(2)}) collective-permute-start(bf16[48,1536]{1,0:T(8,128)(2,1)S(1)} %dynamic-slice_bitcast_fusion.12), channel_id=1, source_target_pairs={{0,16},{2,18},{4,20},{6,22},{8,24},{10,26},{12,28},{14,30},{16,0},... | collective-permute-start | bytes 442376 | tf_op jit(solution)/shard_map/ppermute | solution.py:217
  619.3 12.5 %collective-permute-start.21 = (bf16[48,1536]{1,0:T(8,128)(2,1)S(1)}, bf16[48,1536]{1,0:T(8,128)(2,1)S(1)}, u32[]{:S(2)}, u32[]{:S(2)}) collective-permute-start(bf16[48,1536]{1,0:T(8,128)(2,1)S(1)} %dynamic-slice_bitcast_fusion.13), channel_id=1, source_target_pairs={{0,16},{2,18},{4,20},{6,22},{8,24},{10,26},{12,28},{14,30},{16,0},... | collective-permute-start | bytes 442376 | tf_op jit(solution)/shard_map/ppermute | solution.py:217
  619.5 21.0 %collective-permute-start.16 = (bf16[48,3072]{1,0:T(8,128)(2,1)S(1)}, bf16[48,3072]{1,0:T(8,128)(2,1)S(1)}, u32[]{:S(2)}, u32[]{:S(2)}) collective-permute-start(bf16[48,3072]{1,0:T(8,128)(2,1)S(1)} %fusion.60), channel_id=1, source_target_pairs={{0,1},{1,0},{2,3},{3,2},{4,5},{5,4},{6,7},{7,6},{8,9},{9,8},{10,11... | collective-permute-start | bytes 884744 | tf_op jit(solution)/shard_map/ppermute | solution.py:217
  631.8 6.2 collective-permute-start.22
  633.4 9.5 %copy-start.1 = (bf16[768,768]{1,0:T(8,128)(2,1)S(1)}, bf16[768,768]{1,0:T(8,128)(2,1)}, u32[]{:S(2)}) copy-start(bf16[768,768]{1,0:T(8,128)(2,1)} %param.34) | copy-start | bytes 3538948
  633.5 6.1 collective-permute-start.28
  (63 other events, 263.4 us)
